TPU v7x, 32 devices: a whole 2x2x4 slice. The times are simulated.
32 devices in a mesh: seq: 4 (over x, core), expert: 8 (over z, y).
Axes of the slice: x: 2, y: 2, z: 4, core: 2. Of those that a mesh axis runs over, the one named last changes fastest.
Arguments:
- hidden_in: bfloat16 [4096, 2048], P(('seq', 'expert')), may hold values from -6 to 6
- d_output: bfloat16 [4096, 2048], P(('seq', 'expert')), may hold values from -6 to 6
- gain: float32 [2048], replicated, may hold values from 0.5 to 1.5
- route_ids: int32 [4096, 4], P(('seq', 'expert')), may hold values from 0 to 31, all different within a row; in each aligned block of 128 rows (0 to 127, 128 to 255, ...) at most 24 rows name the same one
- gates: bfloat16 [4096, 4], P(('seq', 'expert')), may hold values from 0.049804688 to 0.59765625
- w_gate: bfloat16 [32, 2048, 768], P(('seq', 'expert')), may hold values from -0.125 to 0.125
- w_up: bfloat16 [32, 2048, 768], P(('seq', 'expert')), may hold values from -0.125 to 0.125
- w_down: bfloat16 [32, 768, 2048], P(('seq', 'expert')), may hold values from -0.21875 to 0.21875
Outputs:
- d_hidden_in: bfloat16 [4096, 2048], P(('seq', 'expert'))
- d_gain: float32 [2048], P(('seq', 'expert'))
- d_gates: bfloat16 [4096, 4], P(('seq', 'expert'))
- d_w_gate: bfloat16 [32, 2048, 768], P(('seq', 'expert'))
- d_w_up: bfloat16 [32, 2048, 768], P(('seq', 'expert'))
- d_w_down: bfloat16 [32, 768, 2048], P(('seq', 'expert'))
Inputs may be any that keep to these rules, and one draw needn't show every extreme that they name: `route_ids`: each row names 4 different experts. Within the 128 rows of one device no expert is named by more than 24 rows, and in every draw some expert is named by exactly 24 rows of some device.
All inputs are finite; a program needn't handle non-finite values.
Results may differ from a plain program's by a relative error of at most 0.0073.
Values may be sent and summed in bfloat16 or wider, within the bound.
A program may use at most 128 MiB of HBM per device.

v0:
```python
import jax
import jax.numpy as jnp
from jax import lax
from jax.sharding import PartitionSpec as P


def slot_index(block_ids, experts, capacity):
    flat_ids = block_ids.reshape(-1)
    onehot = (flat_ids[:, None] == jnp.arange(experts, dtype=jnp.int32)[None, :]).astype(jnp.int32)
    before = jnp.cumsum(onehot, axis=0) - onehot
    position = jnp.sum(before * onehot, axis=1)
    return flat_ids * capacity + position


def expert_backward(rows_in, rows_cot, rows_gate, gate_w, up_w, down_w):
    pre_gate = jnp.dot(rows_in, gate_w, preferred_element_type=jnp.float32)
    pre_up = jnp.dot(rows_in, up_w, preferred_element_type=jnp.float32)
    sigmoid_gate = jax.nn.sigmoid(pre_gate)
    silu_gate = pre_gate * sigmoid_gate
    act = (silu_gate * pre_up).astype(jnp.bfloat16)
    expert_out = jnp.dot(act, down_w, preferred_element_type=jnp.float32)
    slot_grad = jnp.sum(rows_cot.astype(jnp.float32) * expert_out, axis=1).astype(jnp.bfloat16)
    d_expert = (rows_gate.astype(jnp.float32)[:, None] * rows_cot.astype(jnp.float32)).astype(
        jnp.bfloat16
    )
    d_act = lax.dot_general(
        d_expert, down_w, (((1,), (1,)), ((), ())), preferred_element_type=jnp.float32
    )
    grad_gate = (d_act * pre_up * sigmoid_gate * (1.0 + pre_gate * (1.0 - sigmoid_gate))).astype(
        jnp.bfloat16
    )
    grad_up = (d_act * silu_gate).astype(jnp.bfloat16)
    grad_down_w = lax.dot_general(
        act, d_expert, (((0,), (0,)), ((), ())), preferred_element_type=jnp.float32
    ).astype(jnp.bfloat16)
    grad_gate_w = lax.dot_general(
        rows_in, grad_gate, (((0,), (0,)), ((), ())), preferred_element_type=jnp.float32
    ).astype(jnp.bfloat16)
    grad_up_w = lax.dot_general(
        rows_in, grad_up, (((0,), (0,)), ((), ())), preferred_element_type=jnp.float32
    ).astype(jnp.bfloat16)
    d_rows = (
        lax.dot_general(
            grad_gate, gate_w, (((1,), (1,)), ((), ())), preferred_element_type=jnp.float32
        )
        + lax.dot_general(
            grad_up, up_w, (((1,), (1,)), ((), ())), preferred_element_type=jnp.float32
        )
    ).astype(jnp.bfloat16)
    return (d_rows, slot_grad, grad_gate_w, grad_up_w, grad_down_w)


def body(hidden_in, d_output, gain, route_ids, gates, w_gate, w_up, w_down):
    tok_rows, width = hidden_in.shape
    top_count = route_ids.shape[1]
    local_experts = w_gate.shape[0]
    devices = lax.axis_size(("seq", "expert"))
    experts = local_experts * devices
    capacity = max(2, tok_rows * top_count * 3 // (2 * experts))
    block_rows = local_experts * capacity
    wide_rows = hidden_in.astype(jnp.float32)
    inverse_rms = lax.rsqrt(jnp.mean(wide_rows * wide_rows, axis=1, keepdims=True) + 1e-06)
    unit_rows = wide_rows * inverse_rms
    normed = (unit_rows * gain[None, :]).astype(jnp.bfloat16)
    flat_slots = slot_index(route_ids, experts, capacity)
    pair_in = jnp.broadcast_to(normed[:, None, :], (tok_rows, top_count, width)).reshape(-1, width)
    pair_cot = jnp.broadcast_to(d_output[:, None, :], (tok_rows, top_count, width)).reshape(
        -1, width
    )
    send_in = jnp.zeros((experts * capacity, width), jnp.bfloat16).at[flat_slots].set(pair_in)
    send_cot = jnp.zeros((experts * capacity, width), jnp.bfloat16).at[flat_slots].set(pair_cot)
    send_gate = jnp.zeros((experts * capacity,), jnp.bfloat16).at[flat_slots].set(gates.reshape(-1))
    send_in = send_in.reshape(devices, block_rows, width)
    send_cot = send_cot.reshape(devices, block_rows, width)
    send_gate = send_gate.reshape(devices, block_rows)
    got_in, got_cot, got_gate = (
        lax.all_to_all(send_in, ("seq", "expert"), split_axis=0, concat_axis=0, tiled=True),
        lax.all_to_all(send_cot, ("seq", "expert"), split_axis=0, concat_axis=0, tiled=True),
        lax.all_to_all(send_gate, ("seq", "expert"), split_axis=0, concat_axis=0, tiled=True),
    )
    expert_in = (
        got_in.reshape(devices, local_experts, capacity, width)
        .transpose(1, 0, 2, 3)
        .reshape(local_experts, devices * capacity, width)
    )
    expert_cot = (
        got_cot.reshape(devices, local_experts, capacity, width)
        .transpose(1, 0, 2, 3)
        .reshape(local_experts, devices * capacity, width)
    )
    expert_gate = (
        got_gate.reshape(devices, local_experts, capacity)
        .transpose(1, 0, 2)
        .reshape(local_experts, devices * capacity)
    )
    rows_list, grads_list, gate_list, up_list, down_list = ([], [], [], [], [])
    d_rows, slot_grad, grad_gate_w, grad_up_w, grad_down_w = expert_backward(
        expert_in[0], expert_cot[0], expert_gate[0], w_gate[0], w_up[0], w_down[0]
    )
    rows_list.append(d_rows)
    grads_list.append(slot_grad)
    gate_list.append(grad_gate_w)
    up_list.append(grad_up_w)
    down_list.append(grad_down_w)
    d_w_gate = jnp.stack(gate_list)
    d_w_up = jnp.stack(up_list)
    d_w_down = jnp.stack(down_list)
    back_rows = (
        jnp.stack(rows_list)
        .reshape(local_experts, devices, capacity, width)
        .transpose(1, 0, 2, 3)
        .reshape(devices, block_rows, width)
    )
    back_grad = (
        jnp.stack(grads_list)
        .reshape(local_experts, devices, capacity)
        .transpose(1, 0, 2)
        .reshape(devices, block_rows)
    )
    home_rows, home_grad = (
        lax.all_to_all(back_rows, ("seq", "expert"), split_axis=0, concat_axis=0, tiled=True),
        lax.all_to_all(back_grad, ("seq", "expert"), split_axis=0, concat_axis=0, tiled=True),
    )
    pair_rows = home_rows.reshape(experts * capacity, width)[flat_slots]
    d_normed = jnp.sum(pair_rows.reshape(tok_rows, top_count, width).astype(jnp.float32), axis=1)
    d_gates = home_grad.reshape(experts * capacity)[flat_slots].reshape(tok_rows, top_count)
    gain_term = jnp.sum(d_normed * unit_rows, axis=0)
    d_gain = lax.psum_scatter(gain_term, ("seq", "expert"), scatter_dimension=0, tiled=True)
    d_unit = d_normed * gain[None, :]
    inner = jnp.mean(d_unit * unit_rows, axis=1, keepdims=True)
    d_hidden_in = (
        d_output.astype(jnp.float32) + inverse_rms * (d_unit - unit_rows * inner)
    ).astype(jnp.bfloat16)
    return (d_hidden_in, d_gain, d_gates, d_w_gate, d_w_up, d_w_down)


def solution(mesh):
    return jax.shard_map(
        body,
        mesh=mesh,
        in_specs=(
            P(("seq", "expert"), None),
            P(("seq", "expert"), None),
            P(),
            P(("seq", "expert"), None),
            P(("seq", "expert"), None),
            P(("seq", "expert"), None, None),
            P(("seq", "expert"), None, None),
            P(("seq", "expert"), None, None),
        ),
        out_specs=(
            P(("seq", "expert"), None),
            P(("seq", "expert")),
            P(("seq", "expert"), None),
            P(("seq", "expert"), None, None),
            P(("seq", "expert"), None, None),
            P(("seq", "expert"), None, None),
        ),
        check_vma=False,
    )
```

profile of v0, /device:TPU:0, one launch (start us, length us, event | category | flops | bytes accessed | tf_op | source)
XLA Modules:
  0.0 363.6 jit_solution(10889155370512327381)
XLA Ops:
  5.2 3.8 %scatter_custom_fusion = bf16[768]{0:T(1024)(128)(2,1)S(1)} fusion(s32[512]{0:T(512)S(1)} %bitcast.76, bf16[512]{0:T(512)(128)(2,1)S(1)} %reshape.171, bf16[]{:T(256)} %constant.5.clone.1), kind=kCustom, calls=%fused_computation.63 | custom fusion | bytes 1538 | tf_op jit(solution)/shard_map/scatter | solution.py:72
  9.7 7.3 %all-to-all-start = ((bf16[32,1,24]{2,1,0:T(2,128)(2,1)}), bf16[32,1,24]{2,1,0:T(2,128)(2,1)S(1)}, u32[]{:S(2)}, u32[]{:S(2)}) async-start(bf16[32,1,24]{2,1,0:T(2,128)(2,1)} %all_to_all.25), calls=%async_computation | async-start | bytes 32768 | tf_op jit(solution)/shard_map/all_to_all | solution.py:79
  17.0 3.4 broadcast_in_dim.7
  20.4 3.9 %reshape.179 = bf16[512,2048]{1,0:T(8,128)(2,1)} reshape(bf16[128,4,2048]{2,1,0:T(4,128)(2,1)} %broadcast_in_dim.7) | data formatting | bytes 4194304 | tf_op jit(solution)/shard_map/reshape | solution.py:67
  24.4 6.7 %scatter_custom_fusion.1 = bf16[768,2048]{1,0:T(8,128)(2,1)} fusion(s32[512]{0:T(512)S(1)} %bitcast.77, bf16[512,2048]{1,0:T(8,128)(2,1)} %reshape.179, bf16[]{:T(256)} %constant.5.clone.1), kind=kCustom, calls=%fused_computation.35 | custom fusion | bytes 3146240 | tf_op jit(solution)/shard_map/scatter | solution.py:71
  31.1 17.5 %all-to-all-start.1 = ((bf16[32,24,2048]{2,1,0:T(8,128)(2,1)}), bf16[32,24,2048]{2,1,0:T(8,128)(2,1)}, u32[]{:S(2)}, u32[]{:S(2)}) async-start(bf16[32,24,2048]{2,1,0:T(8,128)(2,1)} %bitcast.71), calls=%async_computation.1 | async-start | bytes 6291456 | tf_op jit(solution)/shard_map/all_to_all | solution.py:78
  51.1 2.4 broadcast_in_dim.8
  53.5 3.9 %reshape.187 = bf16[512,2048]{1,0:T(8,128)(2,1)} reshape(bf16[128,4,2048]{2,1,0:T(4,128)(2,1)} %broadcast_in_dim.8) | data formatting | bytes 4194304 | tf_op jit(solution)/shard_map/reshape | solution.py:66
  57.5 6.7 %scatter_custom_fusion.2 = bf16[768,2048]{1,0:T(8,128)(2,1)} fusion(s32[512]{0:T(512)S(1)} %bitcast.78, bf16[512,2048]{1,0:T(8,128)(2,1)} %reshape.187, bf16[]{:T(256)} %constant.5.clone.1), kind=kCustom, calls=%fused_computation.33 | custom fusion | bytes 3146240 | tf_op jit(solution)/shard_map/scatter | solution.py:70
  64.2 57.2 %all-to-all-done.1 = bf16[32,24,2048]{2,1,0:T(8,128)(2,1)} async-done(((bf16[32,24,2048]{2,1,0:T(8,128)(2,1)}), bf16[32,24,2048]{2,1,0:T(8,128)(2,1)}, u32[]{:S(2)}, u32[]{:S(2)}) %all-to-all-start.1) | async-done | bytes 3145760 | tf_op jit(solution)/shard_map/all_to_all | solution.py:78
  121.3 3.5 all-to-all-start.2
  124.9 2.6 fusion
  127.8 4.1 %fusion.11 = f32[768,768]{1,0:T(8,128)} fusion(bf16[768,2048]{1,0:T(8,128)(2,1)S(1)} %bitcast.74, bf16[1,768,2048]{2,1,0:T(8,128)(2,1)S(1)} %copy-done.4), kind=kOutput, calls=%fused_computation.23 | convolution fusion | flops 2415919104 | bytes 8650752 | tf_op jit(solution)/shard_map/dot_general | solution.py:26
  131.8 66.1 %all-to-all-done.2 = bf16[32,24,2048]{2,1,0:T(8,128)(2,1)} async-done(((bf16[32,24,2048]{2,1,0:T(8,128)(2,1)}), bf16[32,24,2048]{2,1,0:T(8,128)(2,1)}, u32[]{:S(2)}, u32[]{:S(2)}) %all-to-all-start.2) | async-done | bytes 3145760 | tf_op jit(solution)/shard_map/all_to_all | solution.py:77
  197.9 5.6 %fusion.5 = f32[768,768]{1,0:T(8,128)S(1)} fusion(bf16[768,2048]{1,0:T(8,128)(2,1)} %bitcast.8, bf16[1,2048,768]{2,1,0:T(8,128)(2,1)} %param.13), kind=kOutput, calls=%fused_computation.17 | convolution fusion | flops 2415919104 | bytes 8650752 | tf_op jit(solution)/shard_map/dot_general | solution.py:16
  203.5 6.3 %multiply_convert_fusion = (bf16[768,768]{1,0:T(8,128)(2,1)S(1)}, bf16[768,768]{1,0:T(8,128)(2,1)S(1)}, bf16[768,768]{1,0:T(8,128)(2,1)}) fusion(f32[768,768]{1,0:T(8,128)S(1)} %fusion.5, f32[768,768]{1,0:T(8,128)S(1)} %copy-done.7, bf16[768,2048]{1,0:T(8,128)(2,1)} %bitcast.8, bf16[1,2048,768]{2,1,0:T(8,128)(2,1)S(1)} %copy-done), kind=kOutput, calls=%fused_computation.28 | convolution fusion | flops 2424766464 | bytes 14548992 | tf_op jit(solution)/shard_map/dot_general | solution.py:17
  209.8 4.5 %fusion.3 = f32[768,2048]{1,0:T(8,128)} fusion(bf16[768,768]{1,0:T(8,128)(2,1)S(1)} %get-tuple-element.21, bf16[1,2048,768]{2,1,0:T(8,128)(2,1)S(1)} %copy-done.3), kind=kOutput, calls=%fused_computation.15 | convolution fusion | flops 2415919104 | bytes 10616832 | tf_op jit(solution)/shard_map/dot_general | solution.py:43
  214.3 4.4 %fusion.1 = bf16[768]{0:T(1024)(128)(2,1)S(1)} fusion(bf16[32,24,2048]{2,1,0:T(8,128)(2,1)} %all-to-all-done.1, bf16[768,768]{1,0:T(8,128)(2,1)S(1)} %get-tuple-element.20, bf16[1,768,2048]{2,1,0:T(8,128)(2,1)S(1)} %copy-done.5), kind=kOutput, calls=%fused_computation.9 | convolution fusion | flops 2420636928 | bytes 7472640 | tf_op jit(solution)/shard_map/dot_general | solution.py:21
  219.4 2.5 all-to-all-start.4
  221.9 6.2 %add_convert_fusion = bf16[768,2048]{1,0:T(8,128)(2,1)} fusion(f32[768,2048]{1,0:T(8,128)} %fusion.3, bf16[768,768]{1,0:T(8,128)(2,1)} %get-tuple-element.22, bf16[1,2048,768]{2,1,0:T(8,128)(2,1)S(1)} %copy-done), kind=kOutput, calls=%fused_computation.11 | convolution fusion | flops 2419064832 | bytes 13762560 | tf_op jit(solution)/shard_map/dot_general | solution.py:46
  229.0 5.2 %all-to-all-start.3 = ((bf16[32,24,2048]{2,1,0:T(8,128)(2,1)}), bf16[32,24,2048]{2,1,0:T(8,128)(2,1)S(1)}, u32[]{:S(2)}, u32[]{:S(2)}) async-start(bf16[32,24,2048]{2,1,0:T(8,128)(2,1)} %bitcast.73), calls=%async_computation.3 | async-start | bytes 6291456 | tf_op jit(solution)/shard_map/all_to_all | solution.py:121
  234.4 6.7 %fusion.13 = bf16[1,2048,768]{2,1,0:T(8,128)(2,1)} fusion(bf16[768,2048]{1,0:T(8,128)(2,1)} %bitcast.8, bf16[768,768]{1,0:T(8,128)(2,1)} %copy-done.6), kind=kOutput, calls=%fused_computation.25 | convolution fusion | flops 2417491968 | bytes 7471104 | tf_op jit(solution)/shard_map/dot_general | solution.py:36
  241.1 6.2 %fusion.14 = bf16[1,2048,768]{2,1,0:T(8,128)(2,1)} fusion(bf16[768,2048]{1,0:T(8,128)(2,1)} %bitcast.8, bf16[768,768]{1,0:T(8,128)(2,1)S(1)} %copy-done.10), kind=kOutput, calls=%fused_computation.26 | convolution fusion | flops 2417491968 | bytes 7471104 | tf_op jit(solution)/shard_map/dot_general | solution.py:39
  247.3 2.6 fusion.2
  249.9 4.0 %fusion.15 = bf16[1,768,2048]{2,1,0:T(8,128)(2,1)} fusion(bf16[768,768]{1,0:T(8,128)(2,1)S(1)} %copy-done.9, bf16[768,2048]{1,0:T(8,128)(2,1)S(1)} %fusion.2), kind=kOutput, calls=%fused_computation.27 | convolution fusion | flops 2417491968 | bytes 7471104 | tf_op jit(solution)/shard_map/dot_general | solution.py:33
  254.0 3.5 gather_fusion.1
  258.3 48.6 %all-to-all-done.3 = bf16[32,24,2048]{2,1,0:T(8,128)(2,1)S(1)} async-done(((bf16[32,24,2048]{2,1,0:T(8,128)(2,1)}), bf16[32,24,2048]{2,1,0:T(8,128)(2,1)S(1)}, u32[]{:S(2)}, u32[]{:S(2)}) %all-to-all-start.3) | async-done | bytes 3145760 | tf_op jit(solution)/shard_map/all_to_all | solution.py:121
  307.0 3.3 gather_fusion
  310.3 5.0 %reshape.148 = f32[128,4,2048]{2,1,0:T(4,128)} reshape(bf16[512,2048]{1,0:T(8,128)(2,1)} %gather_fusion) | data formatting | bytes 6291456 | tf_op jit(solution)/shard_map/convert_element_type | solution.py:125
  315.3 6.0 %reduce_sum.59 = f32[128,2048]{1,0:T(8,128)} reduce(f32[128,4,2048]{2,1,0:T(4,128)} %reshape.148, f32[]{:T(128)} %constant.8.clone.1), dimensions={1}, to_apply=%region_7.8 | reduce | flops 786432 | bytes 5242884 | tf_op jit(solution)/shard_map/reduce_sum | solution.py:125
  323.0 2.7 fusion.30
  325.7 36.9 %all-reduce = f32[2048]{0:T(1024)S(1)} all-reduce(f32[2048]{0:T(1024)S(1)} %get-tuple-element.18), channel_id=2, replica_groups=mesh['seq'=4,'expert'=8] {'seq','expert'}, use_global_device_ids=true, to_apply=%region_10.11.clone | all-reduce | flops 2048 | bytes 16384
  (55 shorter events, 12.9 us)
Async XLA Ops:
  0.6 202.8 %copy-start = (bf16[1,2048,768]{2,1,0:T(8,128)(2,1)S(1)}, bf16[1,2048,768]{2,1,0:T(8,128)(2,1)}, u32[]{:S(2)}) copy-start(bf16[1,2048,768]{2,1,0:T(8,128)(2,1)} %param.14) | copy-start | bytes 9437188
  9.7 21.4 %all-to-all-start = ((bf16[32,1,24]{2,1,0:T(2,128)(2,1)}), bf16[32,1,24]{2,1,0:T(2,128)(2,1)S(1)}, u32[]{:S(2)}, u32[]{:S(2)}) async-start(bf16[32,1,24]{2,1,0:T(2,128)(2,1)} %all_to_all.25), calls=%async_computation | async-start | bytes 32768 | tf_op jit(solution)/shard_map/all_to_all | solution.py:79
  31.1 18.8 %copy-start.2 = (f32[2048]{0:T(1024)S(1)}, f32[2048]{0:T(1024)}, u32[]{:S(2)}) copy-start(f32[2048]{0:T(1024)} %param.10) | copy-start | bytes 24580
  31.1 90.3 %all-to-all-start.1 = ((bf16[32,24,2048]{2,1,0:T(8,128)(2,1)}), bf16[32,24,2048]{2,1,0:T(8,128)(2,1)}, u32[]{:S(2)}, u32[]{:S(2)}) async-start(bf16[32,24,2048]{2,1,0:T(8,128)(2,1)} %bitcast.71), calls=%async_computation.1 | async-start | bytes 6291456 | tf_op jit(solution)/shard_map/all_to_all | solution.py:78
  121.3 76.5 %all-to-all-start.2 = ((bf16[32,24,2048]{2,1,0:T(8,128)(2,1)}), bf16[32,24,2048]{2,1,0:T(8,128)(2,1)}, u32[]{:S(2)}, u32[]{:S(2)}) async-start(bf16[32,24,2048]{2,1,0:T(8,128)(2,1)} %bitcast.72), calls=%async_computation.2 | async-start | bytes 6291456 | tf_op jit(solution)/shard_map/all_to_all | solution.py:77
  124.9 2.8 copy-start.4
  197.9 5.6 %copy-start.7 = (f32[768,768]{1,0:T(8,128)S(1)}, f32[768,768]{1,0:T(8,128)}, u32[]{:S(2)}) copy-start(f32[768,768]{1,0:T(8,128)} %fusion.11) | copy-start | bytes 7077892
  203.5 6.3 %copy-start.3 = (bf16[1,2048,768]{2,1,0:T(8,128)(2,1)S(1)}, bf16[1,2048,768]{2,1,0:T(8,128)(2,1)}, u32[]{:S(2)}) copy-start(bf16[1,2048,768]{2,1,0:T(8,128)(2,1)} %param.13) | copy-start | bytes 9437188
  209.8 4.5 %copy-start.6 = (bf16[768,768]{1,0:T(8,128)(2,1)}, bf16[768,768]{1,0:T(8,128)(2,1)S(1)}, u32[]{:S(2)}) copy-start(bf16[768,768]{1,0:T(8,128)(2,1)S(1)} %get-tuple-element.21) | copy-start | bytes 3538948
  209.8 4.5 %copy-start.8 = (bf16[768,768]{1,0:T(8,128)(2,1)}, bf16[768,768]{1,0:T(8,128)(2,1)S(1)}, u32[]{:S(2)}) copy-start(bf16[768,768]{1,0:T(8,128)(2,1)S(1)} %get-tuple-element.20) | copy-start | bytes 3538948
  209.8 4.5 %copy-start.5 = (bf16[1,768,2048]{2,1,0:T(8,128)(2,1)S(1)}, bf16[1,768,2048]{2,1,0:T(8,128)(2,1)}, u32[]{:S(2)}) copy-start(bf16[1,768,2048]{2,1,0:T(8,128)(2,1)} %param.15) | copy-start | bytes 9437188
  219.4 9.6 %all-to-all-start.4 = ((bf16[32,1,24]{2,1,0:T(2,128)(2,1)}), bf16[32,1,24]{2,1,0:T(2,128)(2,1)S(1)}, u32[]{:S(2)}, u32[]{:S(2)}) async-start(bf16[32,1,24]{2,1,0:T(2,128)(2,1)} %convert_element_type.125), calls=%async_computation.4 | async-start | bytes 32768 | tf_op jit(solution)/shard_map/all_to_all | solution.py:122
  229.0 78.0 %all-to-all-start.3 = ((bf16[32,24,2048]{2,1,0:T(8,128)(2,1)}), bf16[32,24,2048]{2,1,0:T(8,128)(2,1)S(1)}, u32[]{:S(2)}, u32[]{:S(2)}) async-start(bf16[32,24,2048]{2,1,0:T(8,128)(2,1)} %bitcast.73), calls=%async_computation.3 | async-start | bytes 6291456 | tf_op jit(solution)/shard_map/all_to_all | solution.py:121
  234.4 6.7 %copy-start.10 = (bf16[768,768]{1,0:T(8,128)(2,1)S(1)}, bf16[768,768]{1,0:T(8,128)(2,1)}, u32[]{:S(2)}) copy-start(bf16[768,768]{1,0:T(8,128)(2,1)} %get-tuple-element.22) | copy-start | bytes 3538948
  247.3 2.6 copy-start.9
  315.3 47.9 %copy-start.1 = (bf16[1,2048,768]{2,1,0:T(8,128)(2,1)S(1)}, bf16[1,2048,768]{2,1,0:T(8,128)(2,1)}, u32[]{:S(2)}) copy-start(bf16[1,2048,768]{2,1,0:T(8,128)(2,1)} %param.14) | copy-start | bytes 9437188
where the time goes:
time: 367 us; the launch traced here: 364 us
  waiting for transfers between devices  173 us (47%)
  local copies, waits for them, and re-layouts  48.4 us (13%)
  matrix products  48 us (13%)
  blocking collectives  36.9 us (10%)
  starting transfers between devices  36.1 us (10%)
  other arithmetic  20.2 us (6%)
    all_to_all x1, waiting for transfers between devices, body(): lax.all_to_all(send_in, ('seq', 'expert'), split_axis=0, concat_axis=0, t...  66.1 us
    all_to_all x1, waiting for transfers between devices, body(): lax.all_to_all(send_cot, ('seq', 'expert'), split_axis=0, concat_axis=0,...  57.2 us
    all_to_all x1, waiting for transfers between devices, body(): lax.all_to_all(back_rows, ('seq', 'expert'), split_axis=0, concat_axis=0,...  48.6 us
    unnamed x1, blocking collectives  36.9 us
    all_to_all x1, starting transfers between devices, body(): lax.all_to_all(send_cot, ('seq', 'expert'), split_axis=0, concat_axis=0,...  17.5 us
    scatter x2, local copies, waits for them, and re-layouts, body(): jnp.zeros((experts * capacity, width), jnp.bfloat16).at[flat_slots]  13.4 us
  transfers between devices with their start and end apart: 5, of which 4 were waited for; matrix products, arithmetic and copies ran while one was open for 18% of the time, Pallas kernels for 0%

commit v1 on v0

v1 whole, which is shorter than its diff:
```python
import functools

import jax
import jax.numpy as jnp
from jax import lax
from jax.experimental import pallas as pl
from jax.experimental.pallas import tpu as pltpu
from jax.sharding import PartitionSpec as P

BF = jnp.bfloat16
F32 = jnp.float32
AXES = ("seq", "expert")


def coords(outer, inner):
    s = lax.axis_index("seq")
    e = lax.axis_index("expert")
    return s, e // inner, e % inner


def dispatch_kernel(
    seqs, outer, inner, normed, cot, table, got_in, got_cot, table_all,
    line, table_line, stage, line_send, line_recv, table_send, table_recv,
    plane_send, plane_recv, own_sem,
):
    s, o, i = coords(outer, inner)
    plane = seqs * inner
    p = s * inner + i
    width = normed.shape[1]
    cap = got_in.shape[1]
    barrier = pltpu.get_barrier_semaphore()

    def line_peer(d):
        return (s, ((o + d) % outer) * inner + i)

    def plane_peer(t):
        return (t // inner, o * inner + t % inner)

    for d in range(1, outer):
        pl.semaphore_signal(barrier, inc=1, device_id=line_peer(d), device_id_type=pl.DeviceIdType.MESH)

    def greet(q, carry):
        pl.semaphore_signal(
            barrier, inc=1, device_id=plane_peer((p + q) % plane), device_id_type=pl.DeviceIdType.MESH
        )
        return carry

    lax.fori_loop(1, plane, greet, 0)
    pl.semaphore_wait(barrier, outer - 1 + plane - 1)

    def remote(src, dst, send, recv, peer):
        return pltpu.make_async_remote_copy(
            src_ref=src, dst_ref=dst, send_sem=send, recv_sem=recv,
            device_id=peer, device_id_type=pl.DeviceIdType.MESH,
        )

    sources = (cot, normed)
    targets = (got_cot, got_in)

    def table_copy(d):
        return remote(
            table.at[(o + d) % outer], table_line.at[d], table_send.at[d], table_recv.at[d], line_peer(d)
        )

    def line_copy(t, d):
        return remote(sources[t], line.at[t, d], line_send.at[t, d], line_recv.at[t, d], line_peer(d))

    def plane_copy(t, d, q):
        to = (p + q) % plane
        home = s * (outer * inner) + ((o - d + outer) % outer) * inner + i
        return remote(
            stage.at[t, d, to], targets[t].at[home],
            plane_send.at[t, d, q], plane_recv.at[t, d, q], plane_peer(to),
        )

    def own_copy(t, d):
        home = s * (outer * inner) + ((o - d + outer) % outer) * inner + i
        return pltpu.make_async_copy(stage.at[t, d, p], targets[t].at[home], own_sem.at[t, d])

    def table_out(d):
        src = table.at[o] if d == 0 else table_line.at[d]
        return pltpu.make_async_copy(src, table_all.at[d], table_send.at[d] if d == 0 else table_recv.at[d])

    for d in range(1, outer):
        table_copy(d).start()
    for d in range(1, outer):
        for t in range(2):
            line_copy(t, d).start()

    for d in range(outer):
        if d > 0:
            table_copy(d).wait_recv()
        for t in range(2):
            if d > 0:
                line_copy(t, d).wait_recv()
            step = 512 if width % 512 == 0 else width

            def place(c, carry, t=t, d=d, step=step):
                cols = pl.ds(pl.multiple_of(c * step, step), step)
                rows = sources[t][:, cols] if d == 0 else line[t, d, :, cols]
                pick = table[o] if d == 0 else table_line[d]
                put = jnp.dot(pick, rows, preferred_element_type=F32).astype(BF)
                stage[t, d, :, :, cols] = put.reshape(plane, cap, step)
                return carry

            lax.fori_loop(0, width // step, place, 0)
            own_copy(t, d).start()

            def push(q, carry, t=t, d=d):
                plane_copy(t, d, q).start()
                return carry

            lax.fori_loop(1, plane, push, 0)
        table_out(d).start()

    for d in range(1, outer):
        table_copy(d).wait_send()
        for t in range(2):
            line_copy(t, d).wait_send()
    for d in range(outer):
        table_out(d).wait()
        for t in range(2):
            own_copy(t, d).wait()

            def finish(q, carry, t=t, d=d):
                plane_copy(t, d, q).wait_recv()
                plane_copy(t, d, q).wait_send()
                return carry

            lax.fori_loop(1, plane, finish, 0)


def dispatch(normed, cot, table, seqs, outer, inner, cap):
    rows, width = normed.shape
    plane = seqs * inner
    count = plane * outer
    vmem = pl.BlockSpec(memory_space=pltpu.VMEM)
    anywhere = pl.BlockSpec(memory_space=pl.ANY)
    dma = pltpu.SemaphoreType.DMA
    return pl.pallas_call(
        functools.partial(dispatch_kernel, seqs, outer, inner),
        out_shape=(
            jax.ShapeDtypeStruct((count, cap, width), BF),
            jax.ShapeDtypeStruct((count, cap, width), BF),
            jax.ShapeDtypeStruct(table.shape, BF),
        ),
        in_specs=[vmem, vmem, vmem],
        out_specs=(anywhere, anywhere, anywhere),
        scratch_shapes=[
            pltpu.VMEM((2, outer, rows, width), BF),
            pltpu.VMEM(table.shape, BF),
            pltpu.VMEM((2, outer, plane, cap, width), BF),
            dma((2, outer)),
            dma((2, outer)),
            dma((outer,)),
            dma((outer,)),
            dma((2, outer, plane)),
            dma((2, outer, plane)),
            dma((2, outer)),
        ],
        compiler_params=pltpu.CompilerParams(
            collective_id=0, has_side_effects=True, vmem_limit_bytes=40 * 1024 * 1024
        ),
        name="dispatch",
    )(normed, cot, table)


def expert_backward(rows_in, rows_cot, rows_gate, gate_w, up_w, down_w):
    pre_gate = jnp.dot(rows_in, gate_w, preferred_element_type=F32)
    pre_up = jnp.dot(rows_in, up_w, preferred_element_type=F32)
    sigmoid_gate = jax.nn.sigmoid(pre_gate)
    silu_gate = pre_gate * sigmoid_gate
    act = (silu_gate * pre_up).astype(BF)
    expert_out = jnp.dot(act, down_w, preferred_element_type=F32)
    slot_grad = jnp.sum(rows_cot.astype(F32) * expert_out, axis=1).astype(BF)
    d_expert = (rows_gate.astype(F32)[:, None] * rows_cot.astype(F32)).astype(BF)
    d_act = lax.dot_general(d_expert, down_w, (((1,), (1,)), ((), ())), preferred_element_type=F32)
    grad_gate = (d_act * pre_up * sigmoid_gate * (1.0 + pre_gate * (1.0 - sigmoid_gate))).astype(BF)
    grad_up = (d_act * silu_gate).astype(BF)
    turned = (((0,), (0,)), ((), ()))
    grad_down_w = lax.dot_general(act, d_expert, turned, preferred_element_type=F32).astype(BF)
    grad_gate_w = lax.dot_general(rows_in, grad_gate, turned, preferred_element_type=F32).astype(BF)
    grad_up_w = lax.dot_general(rows_in, grad_up, turned, preferred_element_type=F32).astype(BF)
    across = (((1,), (1,)), ((), ()))
    d_rows = (
        lax.dot_general(grad_gate, gate_w, across, preferred_element_type=F32)
        + lax.dot_general(grad_up, up_w, across, preferred_element_type=F32)
    ).astype(BF)
    return (d_rows, slot_grad, grad_gate_w, grad_up_w, grad_down_w)


def body(hidden_in, d_output, gain, route_ids, gates, w_gate, w_up, w_down):
    tok_rows, width = hidden_in.shape
    top_count = route_ids.shape[1]
    seqs = lax.axis_size("seq")
    per_seq = lax.axis_size("expert")
    outer = 4 if per_seq % 4 == 0 else 2
    inner = per_seq // outer
    devices = seqs * per_seq
    experts = w_gate.shape[0] * devices
    capacity = max(2, tok_rows * top_count * 3 // (2 * experts))
    cap = -(-capacity // 8) * 8
    wide_rows = hidden_in.astype(F32)
    inverse_rms = lax.rsqrt(jnp.mean(wide_rows * wide_rows, axis=1, keepdims=True) + 1e-06)
    unit_rows = wide_rows * inverse_rms
    normed = (unit_rows * gain[None, :]).astype(BF)

    ids_t = route_ids.T
    gates_t = gates.T
    names = jnp.arange(experts, dtype=jnp.int32)
    hit = ids_t[:, None, :] == names[None, :, None]
    chosen = jnp.any(hit, axis=0)
    gate_map = jnp.sum(jnp.where(hit, gates_t[:, None, :].astype(F32), 0.0), axis=0)
    token = jnp.arange(tok_rows, dtype=jnp.int32)
    earlier = (token[:, None] < token[None, :]).astype(BF)
    position = jnp.dot(chosen.astype(BF), earlier, preferred_element_type=F32).astype(jnp.int32)
    placed = chosen[:, None, :] & (position[:, None, :] == jnp.arange(cap, dtype=jnp.int32)[None, :, None])
    table = placed.astype(BF)
    send_gate = jnp.sum(jnp.where(placed, gate_map[:, None, :], 0.0), axis=2).astype(BF)
    got_gate = lax.all_to_all(send_gate, AXES, split_axis=0, concat_axis=0, tiled=True)
    by_plane = (
        table.reshape(seqs, outer, inner, cap, tok_rows)
        .transpose(1, 0, 2, 3, 4)
        .reshape(outer, seqs * inner * cap, tok_rows)
    )
    got_in, got_cot, _ = dispatch(normed, d_output, by_plane, seqs, outer, inner, cap)
    d_rows, slot_grad, grad_gate_w, grad_up_w, grad_down_w = expert_backward(
        got_in.reshape(-1, width), got_cot.reshape(-1, width), got_gate.reshape(-1),
        w_gate[0], w_up[0], w_down[0],
    )
    home_grad = lax.all_to_all(
        slot_grad.reshape(devices, cap), AXES, split_axis=0, concat_axis=0, tiled=True
    )
    home_rows = lax.all_to_all(
        d_rows.reshape(devices, cap, width), AXES, split_axis=0, concat_axis=0, tiled=True
    )
    d_normed = lax.dot_general(
        table.reshape(-1, tok_rows), home_rows.reshape(-1, width), (((0,), (0,)), ((), ())),
        preferred_element_type=F32,
    )
    grad_map = jnp.sum(jnp.where(placed, home_grad[:, :, None].astype(F32), 0.0), axis=1)
    d_gates = jnp.sum(jnp.where(hit, grad_map[None], 0.0), axis=1).astype(BF).T
    gain_term = jnp.sum(d_normed * unit_rows, axis=0)
    gain_parts = lax.all_to_all(
        gain_term.reshape(devices, -1), AXES, split_axis=0, concat_axis=0, tiled=True
    )
    d_gain = jnp.sum(gain_parts, axis=0)
    d_unit = d_normed * gain[None, :]
    inner_mean = jnp.mean(d_unit * unit_rows, axis=1, keepdims=True)
    d_hidden_in = (
        d_output.astype(F32) + inverse_rms * (d_unit - unit_rows * inner_mean)
    ).astype(BF)
    return (d_hidden_in, d_gain, d_gates, grad_gate_w[None], grad_up_w[None], grad_down_w[None])


def solution(mesh):
    rows = P(AXES, None)
    blocks = P(AXES, None, None)
    return jax.shard_map(
        body,
        mesh=mesh,
        in_specs=(rows, rows, P(), rows, rows, blocks, blocks, blocks),
        out_specs=(rows, P(AXES), rows, blocks, blocks, blocks),
        check_vma=False,
    )
```

time: 367 us -> 279 us (0.76)
  Pallas kernels: 0 us -> 108 us
  waiting for transfers between devices: 173 us -> 67.4 us
  local copies, waits for them, and re-layouts: 48.4 us -> 5.49 us
  blocking collectives: 36.9 us -> 8.84 us
  other arithmetic: 20.2 us -> 10.9 us
  starting transfers between devices: 36.1 us -> 31.6 us
    pallas_call x0 -> x1, Pallas kernels: none -> 108 us  [dispatch(): pl.pallas_call(functools.partial(dispatch_kernel, seqs, outer, inner), ou...]
    all_to_all x5 -> x3, waiting for transfers between devices: 173 us -> 67.4 us  [the longest x1 55.9 us: body(): lax.all_to_all(d_rows.reshape(devices, cap, width), AXES, split_axis=0, c...]
    unnamed x1 -> x0, blocking collectives: 36.9 us -> none
    scatter x3 -> x0, local copies, waits for them, and re-layouts: 17.2 us -> none  [the longest x2 13.4 us: body(): jnp.zeros((experts * capacity, width), jnp.bfloat16).at[flat_slots]]
    all_to_all x0 -> x1, blocking collectives: none -> 8.84 us  [body(): lax.all_to_all(send_gate, AXES, split_axis=0, concat_axis=0, tiled=True)]
    reshape x5 -> x0, local copies, waits for them, and re-layouts: 8.22 us -> none  [the longest x1 3.94 us: body(): jnp.broadcast_to(normed[:, None, :], (tok_rows, top_count, width))]
    gather x2 -> x0, local copies, waits for them, and re-layouts: 6.84 us -> none  [the longest x1 3.51 us: body(): home_grad.reshape(experts * capacity)[flat_slots]]
    reduce_sum x3 -> x4, other arithmetic: 7.8 us -> 1.44 us  [the longest x1 0.59 us: body(): d_gates = jnp.sum(jnp.where(hit, grad_map[None], 0.0), axis=1).astype(BF).T]
  transfers between devices with their start and end apart: 5 -> 3, of which waited for: 4 -> 3; matrix products, arithmetic and copies ran while one was open for 18% -> 7% of each run, Pallas kernels for 0% -> 0%
where the time goes in v1:
time: 279 us; the launch traced here: 278 us
  Pallas kernels  108 us (39%)
  waiting for transfers between devices  67.4 us (24%)
  matrix products  45.3 us (16%)
  starting transfers between devices  31.6 us (11%)
  other arithmetic  10.9 us (4%)
  blocking collectives  8.84 us (3%)
  local copies, waits for them, and re-layouts  5.49 us (2%)
    pallas_call x1, Pallas kernels, dispatch(): pl.pallas_call(functools.partial(dispatch_kernel, seqs, outer, inner), ou...  108 us
    all_to_all x1, waiting for transfers between devices, body(): lax.all_to_all(d_rows.reshape(devices, cap, width), AXES, split_axis=0, c...  55.9 us
    all_to_all x1, starting transfers between devices, body(): lax.all_to_all(slot_grad.reshape(devices, cap), AXES, split_axis=0, conca...  25.3 us
    all_to_all x1, blocking collectives, body(): lax.all_to_all(send_gate, AXES, split_axis=0, concat_axis=0, tiled=True)  8.84 us
    all_to_all x1, waiting for transfers between devices, body(): lax.all_to_all(slot_grad.reshape(devices, cap), AXES, split_axis=0, conca...  7.02 us
    dot_general x1, matrix products, expert_backward(): pre_gate = jnp.dot(rows_in, gate_w, preferred_element_type=F32)  6.76 us
    dot_general x1, matrix products, expert_backward(): lax.dot_general(rows_in, grad_gate, turned, preferred_element_type=F32)  6.71 us
  transfers between devices with their start and end apart: 3, of which 3 were waited for; matrix products, arithmetic and copies ran while one was open for 7% of the time, Pallas kernels for 0%

profile of v1, /device:TPU:0, one launch (start us, length us, event | category | flops | bytes accessed | tf_op | source)
XLA Modules:
  0.0 278.2 jit_solution(17482777993541879837)
XLA Ops:
  0.6 0.8 fusion.40
  1.7 1.2 fusion.33
  3.0 1.2 fusion.26.normed
  4.4 1.0 copy-done.3
  5.4 107.7 %dispatch.1 = (bf16[32,24,2048]{2,1,0:T(8,128)(2,1)S(1)}, bf16[32,24,2048]{2,1,0:T(8,128)(2,1)S(1)}, bf16[4,192,128]{2,1,0:T(8,128)(2,1)}) custom-call(bf16[128,2048]{1,0:T(8,128)(2,1)S(1)} %fusion.26.normed, bf16[128,2048]{1,0:T(8,128)(2,1)S(1)} %copy-done.3, bf16[4,192,128]{2,1,0:T(8,128)(2,1)S(1)} %fusion.37.table), custom_call_target="tpu_custom_call" | custom-call | tf_op jit(solution)/shard_map/dispatch/pallas_call | solution.py:140
  113.1 6.8 %fusion.5 = f32[768,768]{1,0:T(8,128)S(1)} fusion(bf16[768,2048]{1,0:T(8,128)(2,1)S(1)} %bitcast.77, bf16[1,2048,768]{2,1,0:T(8,128)(2,1)} %param.13), kind=kOutput, calls=%fused_computation.12 | convolution fusion | flops 2415919104 | bytes 8650752 | tf_op jit(solution)/shard_map/dot_general | solution.py:169
  120.0 4.1 %multiply_convert_fusion = (bf16[768,768]{1,0:T(8,128)(2,1)S(1)}, f32[768,768]{1,0:T(8,128)}) fusion(f32[768,768]{1,0:T(8,128)S(1)} %fusion.5, bf16[768,2048]{1,0:T(8,128)(2,1)S(1)} %bitcast.78, bf16[1,2048,768]{2,1,0:T(8,128)(2,1)S(1)} %copy-done), kind=kOutput, calls=%fused_computation.26 | convolution fusion | flops 2419458048 | bytes 12189696 | tf_op jit(solution)/shard_map/dot_general | solution.py:170
  124.1 1.0 copy-done.15
  125.1 2.9 %fusion.1 = bf16[768]{0:T(1024)(128)(2,1)S(1)} fusion(bf16[32,24,2048]{2,1,0:T(8,128)(2,1)S(1)} %get-tuple-element.8, bf16[768,768]{1,0:T(8,128)(2,1)S(1)} %get-tuple-element.16, bf16[1,768,2048]{2,1,0:T(8,128)(2,1)S(1)} %copy-done.9), kind=kOutput, calls=%fused_computation.4 | convolution fusion | flops 2420636928 | bytes 7472640 | tf_op jit(solution)/shard_map/dot_general | solution.py:174
  128.0 0.7 convert_element_type.168
  128.8 25.3 %all-to-all-start.3 = ((bf16[32,1,24]{2,1,0:T(2,128)(2,1)}), bf16[32,1,24]{2,1,0:T(2,128)(2,1)S(1)}, u32[]{:S(2)}, u32[]{:S(2)}) async-start(bf16[32,1,24]{2,1,0:T(2,128)(2,1)} %convert_element_type.168), calls=%async_computation.3 | async-start | bytes 32768 | tf_op jit(solution)/shard_map/all_to_all | solution.py:231
  154.1 7.0 %all-to-all-done.3 = bf16[32,1,24]{2,1,0:T(2,128)(2,1)S(1)} async-done(((bf16[32,1,24]{2,1,0:T(2,128)(2,1)}), bf16[32,1,24]{2,1,0:T(2,128)(2,1)S(1)}, u32[]{:S(2)}, u32[]{:S(2)}) %all-to-all-start.3) | async-done | bytes 1568 | tf_op jit(solution)/shard_map/all_to_all | solution.py:231
  161.6 8.8 %all_to_all.26 = bf16[32,1,24]{2,1,0:T(2,128)(2,1)S(1)} all-to-all(bf16[32,1,24]{2,1,0:T(2,128)(2,1)S(1)} %copy.33), channel_id=1, replica_groups=mesh['seq'=4,'expert'=8] {'seq','expert'}, dimensions={0} | all-to-all | bytes 3072 | tf_op jit(solution)/shard_map/all_to_all | solution.py:220
  170.5 2.6 fusion
  173.3 0.7 copy-done.14
  174.1 4.9 %multiply_convert_fusion.1 = (bf16[768,768]{1,0:T(8,128)(2,1)S(1)}, bf16[768,768]{1,0:T(8,128)(2,1)S(1)}) fusion(f32[768,768]{1,0:T(8,128)S(1)} %copy-done.14, f32[768,768]{1,0:T(8,128)} %get-tuple-element.17, bf16[768,2048]{1,0:T(8,128)(2,1)S(1)} %bitcast.82, bf16[1,768,2048]{2,1,0:T(8,128)(2,1)S(1)} %copy-done.10), kind=kOutput, calls=%fused_computation.27 | convolution fusion | flops 2423586816 | bytes 13369344 | tf_op jit(solution)/shard_map/dot_general | solution.py:177
  179.0 2.6 fusion.3
  181.7 4.1 %add_convert_fusion = bf16[768,2048]{1,0:T(8,128)(2,1)} fusion(f32[768,2048]{1,0:T(8,128)S(1)} %fusion.3, bf16[768,768]{1,0:T(8,128)(2,1)S(1)} %get-tuple-element.14, bf16[1,2048,768]{2,1,0:T(8,128)(2,1)S(1)} %copy-done), kind=kOutput, calls=%fused_computation.6 | convolution fusion | flops 2419064832 | bytes 13762560 | tf_op jit(solution)/shard_map/dot_general | solution.py:187
  185.8 3.7 %all-to-all-start.1 = ((bf16[32,24,2048]{2,1,0:T(8,128)(2,1)}), bf16[32,24,2048]{2,1,0:T(8,128)(2,1)}, u32[]{:S(2)}, u32[]{:S(2)}) async-start(bf16[32,24,2048]{2,1,0:T(8,128)(2,1)} %bitcast.81), calls=%async_computation.1 | async-start | bytes 6291456 | tf_op jit(solution)/shard_map/all_to_all | solution.py:234
  189.5 0.6 select_reduce_fusion.2
  190.3 6.7 %fusion.15 = bf16[1,2048,768]{2,1,0:T(8,128)(2,1)} fusion(bf16[768,2048]{1,0:T(8,128)(2,1)} %bitcast.79, bf16[768,768]{1,0:T(8,128)(2,1)} %copy-done.12), kind=kOutput, calls=%fused_computation.22 | convolution fusion | flops 2417491968 | bytes 7471104 | tf_op jit(solution)/shard_map/dot_general | solution.py:182
  197.0 4.1 %fusion.16 = bf16[1,2048,768]{2,1,0:T(8,128)(2,1)} fusion(bf16[768,2048]{1,0:T(8,128)(2,1)S(1)} %bitcast.80, bf16[768,768]{1,0:T(8,128)(2,1)S(1)} %copy-done.18), kind=kOutput, calls=%fused_computation.23 | convolution fusion | flops 2417491968 | bytes 7471104 | tf_op jit(solution)/shard_map/dot_general | solution.py:183
  201.1 0.6 fusion.2
  201.6 0.7 copy-done.16
  202.3 4.0 %fusion.17 = bf16[1,768,2048]{2,1,0:T(8,128)(2,1)} fusion(bf16[768,768]{1,0:T(8,128)(2,1)S(1)} %copy-done.16, bf16[768,2048]{1,0:T(8,128)(2,1)S(1)} %fusion.2), kind=kOutput, calls=%fused_computation.24 | convolution fusion | flops 2417491968 | bytes 7471104 | tf_op jit(solution)/shard_map/dot_general | solution.py:181
  206.3 55.9 %all-to-all-done.1 = bf16[32,24,2048]{2,1,0:T(8,128)(2,1)} async-done(((bf16[32,24,2048]{2,1,0:T(8,128)(2,1)}), bf16[32,24,2048]{2,1,0:T(8,128)(2,1)}, u32[]{:S(2)}, u32[]{:S(2)}) %all-to-all-start.1) | async-done | bytes 3145760 | tf_op jit(solution)/shard_map/all_to_all | solution.py:234
  262.3 5.0 %fusion.32 = (f32[2048]{0:T(1024)S(1)}, f32[128]{0:T(128)S(1)}, f32[128,2048]{1,0:T(8,128)}) fusion(bf16[128,2048]{1,0:T(8,128)(2,1)} %param.8, f32[128]{0:T(128)S(1)} %add_rsqrt_fusion, f32[2048]{0:T(1024)S(1)} %copy-done.6, bf16[32,24,2048]{2,1,0:T(8,128)(2,1)} %all-to-all-done.1, s32[32,128]{1,0:T(8,128)S(1)} %convolution_convert_fusion.3, ...), kind=kOutput, calls=%fused_computation.44 | convolution fusion | flops 404682624 | bytes 4756480 | tf_op jit(solution)/shard_map/dot_general | solution.py:237
  267.3 0.7 all_to_all.19
  267.9 2.6 all-to-all-start.2
  270.5 2.7 fusion.31
  273.2 4.4 %all-to-all-done.2 = f32[32,1,64]{2,1,0:T(1,128)S(1)} async-done(((f32[32,1,64]{2,1,0:T(1,128)}), f32[32,1,64]{2,1,0:T(1,128)S(1)}, u32[]{:S(2)}, u32[]{:S(2)}) %all-to-all-start.2) | async-done | bytes 8224 | tf_op jit(solution)/shard_map/all_to_all | solution.py:244
  277.6 0.5 reduce_sum.86
  (50 shorter events, 1.3 us)
Async XLA Ops:
  0.6 119.3 %copy-start = (bf16[1,2048,768]{2,1,0:T(8,128)(2,1)S(1)}, bf16[1,2048,768]{2,1,0:T(8,128)(2,1)}, u32[]{:S(2)}) copy-start(bf16[1,2048,768]{2,1,0:T(8,128)(2,1)} %param.14) | copy-start | bytes 9437188
  4.4 1.0 copy-start.3
  113.1 6.8 %copy-start.4 = (bf16[32,24,2048]{2,1,0:T(8,128)(2,1)}, bf16[32,24,2048]{2,1,0:T(8,128)(2,1)S(1)}, u32[]{:S(2)}) copy-start(bf16[32,24,2048]{2,1,0:T(8,128)(2,1)S(1)} %get-tuple-element.9) | copy-start | bytes 9437188
  113.1 10.9 %copy-start.1 = (bf16[32,24,2048]{2,1,0:T(8,128)(2,1)}, bf16[32,24,2048]{2,1,0:T(8,128)(2,1)S(1)}, u32[]{:S(2)}) copy-start(bf16[32,24,2048]{2,1,0:T(8,128)(2,1)S(1)} %get-tuple-element.8) | copy-start | bytes 9437188
  119.9 4.1 %copy-start.13 = (f32[768,768]{1,0:T(8,128)}, f32[768,768]{1,0:T(8,128)S(1)}, u32[]{:S(2)}) copy-start(f32[768,768]{1,0:T(8,128)S(1)} %fusion.5) | copy-start | bytes 7077892
  119.9 5.1 %copy-start.9 = (bf16[1,768,2048]{2,1,0:T(8,128)(2,1)S(1)}, bf16[1,768,2048]{2,1,0:T(8,128)(2,1)}, u32[]{:S(2)}) copy-start(bf16[1,768,2048]{2,1,0:T(8,128)(2,1)} %param.15) | copy-start | bytes 9437188
  124.1 1.0 copy-start.15
  125.1 29.0 %copy-start.8 = (bf16[128,4]{0,1:T(4,128)(2,1)S(1)}, bf16[128,4]{0,1:T(4,128)(2,1)}, u32[]{:S(2)}) copy-start(bf16[128,4]{0,1:T(4,128)(2,1)} %param.12) | copy-start | bytes 3076
  125.1 29.0 %copy-start.7 = (s32[128,4]{0,1:T(4,128)S(1)}, s32[128,4]{0,1:T(4,128)}, u32[]{:S(2)}) copy-start(s32[128,4]{0,1:T(4,128)} %param.11) | copy-start | bytes 6148
  128.8 32.4 %all-to-all-start.3 = ((bf16[32,1,24]{2,1,0:T(2,128)(2,1)}), bf16[32,1,24]{2,1,0:T(2,128)(2,1)S(1)}, u32[]{:S(2)}, u32[]{:S(2)}) async-start(bf16[32,1,24]{2,1,0:T(2,128)(2,1)} %convert_element_type.168), calls=%async_computation.3 | async-start | bytes 32768 | tf_op jit(solution)/shard_map/all_to_all | solution.py:231
  170.5 2.8 %copy-start.10 = (bf16[1,768,2048]{2,1,0:T(8,128)(2,1)S(1)}, bf16[1,768,2048]{2,1,0:T(8,128)(2,1)}, u32[]{:S(2)}) copy-start(bf16[1,768,2048]{2,1,0:T(8,128)(2,1)} %param.15) | copy-start | bytes 9437188
  170.5 3.6 %copy-start.14 = (f32[768,768]{1,0:T(8,128)S(1)}, f32[768,768]{1,0:T(8,128)}, u32[]{:S(2)}) copy-start(f32[768,768]{1,0:T(8,128)} %copy-done.13) | copy-start | bytes 7077892
  174.1 4.9 %copy-start.11 = (bf16[1,2048,768]{2,1,0:T(8,128)(2,1)S(1)}, bf16[1,2048,768]{2,1,0:T(8,128)(2,1)}, u32[]{:S(2)}) copy-start(bf16[1,2048,768]{2,1,0:T(8,128)(2,1)} %param.13) | copy-start | bytes 9437188
  179.0 2.7 copy-start.12
  179.0 2.7 copy-start.17
  185.8 76.5 %all-to-all-start.1 = ((bf16[32,24,2048]{2,1,0:T(8,128)(2,1)}), bf16[32,24,2048]{2,1,0:T(8,128)(2,1)}, u32[]{:S(2)}, u32[]{:S(2)}) async-start(bf16[32,24,2048]{2,1,0:T(8,128)(2,1)} %bitcast.81), calls=%async_computation.1 | async-start | bytes 6291456 | tf_op jit(solution)/shard_map/all_to_all | solution.py:234
  190.2 6.7 %copy-start.5 = (bf16[32,24,2048]{2,1,0:T(8,128)(2,1)S(1)}, bf16[32,24,2048]{2,1,0:T(8,128)(2,1)}, u32[]{:S(2)}) copy-start(bf16[32,24,2048]{2,1,0:T(8,128)(2,1)} %copy-done.4) | copy-start | bytes 9437188
  190.2 6.7 %copy-start.18 = (bf16[768,768]{1,0:T(8,128)(2,1)S(1)}, bf16[768,768]{1,0:T(8,128)(2,1)}, u32[]{:S(2)}) copy-start(bf16[768,768]{1,0:T(8,128)(2,1)} %copy-done.17) | copy-start | bytes 3538948
  197.0 4.1 %copy-start.2 = (bf16[32,24,2048]{2,1,0:T(8,128)(2,1)S(1)}, bf16[32,24,2048]{2,1,0:T(8,128)(2,1)}, u32[]{:S(2)}) copy-start(bf16[32,24,2048]{2,1,0:T(8,128)(2,1)} %copy-done.1) | copy-start | bytes 9437188
  201.1 1.3 copy-start.16
  202.3 60.0 %copy-start.6 = (f32[2048]{0:T(1024)S(1)}, f32[2048]{0:T(1024)}, u32[]{:S(2)}) copy-start(f32[2048]{0:T(1024)} %param.10) | copy-start | bytes 24580
  267.9 9.7 %all-to-all-start.2 = ((f32[32,1,64]{2,1,0:T(1,128)}), f32[32,1,64]{2,1,0:T(1,128)S(1)}, u32[]{:S(2)}, u32[]{:S(2)}) async-start(f32[32,1,64]{2,1,0:T(1,128)} %all_to_all.19), calls=%async_computation.2 | async-start | bytes 32768 | tf_op jit(solution)/shard_map/all_to_all | solution.py:244

commit v2 on v1

v2 whole, which is shorter than its diff:
```python
import functools

import jax
import jax.numpy as jnp
from jax import lax
from jax.experimental import pallas as pl
from jax.experimental.pallas import tpu as pltpu
from jax.sharding import PartitionSpec as P

BF = jnp.bfloat16
F32 = jnp.float32
AXES = ("seq", "expert")


def coords(outer, inner):
    s = lax.axis_index("seq")
    e = lax.axis_index("expert")
    return s, e // inner, e % inner


LANES = 128
MESH = pl.DeviceIdType.MESH


def remote(src, dst, send, recv, peer):
    return pltpu.make_async_remote_copy(
        src_ref=src, dst_ref=dst, send_sem=send, recv_sem=recv, device_id=peer, device_id_type=MESH
    )


def greet_all(s, o, i, seqs, outer, inner):
    barrier = pltpu.get_barrier_semaphore()
    plane = seqs * inner
    p = s * inner + i
    for ok, step in ((o > 0, -1), (o < outer - 1, 1)):

        @pl.when(ok)
        def _():
            pl.semaphore_signal(
                barrier, inc=1, device_id=(s, (o + step) * inner + i), device_id_type=MESH
            )

    def greet(q, carry):
        to = (p + q) % plane
        pl.semaphore_signal(
            barrier, inc=1, device_id=(to // inner, o * inner + to % inner), device_id_type=MESH
        )
        return carry

    lax.fori_loop(1, plane, greet, 0)
    beside = (o > 0).astype(jnp.int32) + (o < outer - 1).astype(jnp.int32)
    pl.semaphore_wait(barrier, plane - 1 + beside)


def dispatch_kernel(
    seqs, outer, inner, normed, cot, table, got_in, got_cot, table_all,
    line, table_line, stage_cot, stage_in, line_send, line_recv, table_send, table_recv,
    plane_send, plane_recv, own_sem, out_sem,
):
    s, o, i = coords(outer, inner)
    plane = seqs * inner
    p = s * inner + i
    width = normed.shape[1]
    cap = got_in.shape[1]
    greet_all(s, o, i, seqs, outer, inner)

    sources = (cot, normed)
    stages = (stage_cot, stage_in)
    targets = (got_cot, got_in)

    def hop(kind, src, way, own):
        peer = (s, (o + 1 - 2 * way) * inner + i)
        if kind == 2:
            held = table if own else table_line.at[src]
            return remote(held, table_line.at[src], table_send.at[src, way], table_recv.at[src], peer)
        held = sources[kind] if own else line.at[kind, src]
        return remote(
            held, line.at[kind, src], line_send.at[kind, src, way], line_recv.at[kind, src], peer
        )

    def plane_copy(t, src, q):
        to = (p + q) % plane
        home = s * (outer * inner) + src * inner + i
        return remote(
            stages[t].at[src, to], targets[t].at[home],
            plane_send.at[t, src, q], plane_recv.at[t, src, q],
            (to // inner, o * inner + to % inner),
        )

    def own_copy(t, src):
        home = s * (outer * inner) + src * inner + i
        return pltpu.make_async_copy(stages[t].at[src, p], targets[t].at[home], own_sem.at[t, src])

    def table_out(src, own):
        held = table.at[o] if own else table_line.at[src, o]
        return pltpu.make_async_copy(held, table_all.at[src], out_sem.at[src])

    def place(t, src, own):
        step = 512 if width % 512 == 0 else width
        pick = (table[o] if own else table_line[src, o]).astype(F32)
        mark = jnp.where(pick != 0.0, 1.0, 0.0).astype(BF)
        if t == 0:
            gate = jnp.broadcast_to(jnp.sum(pick, axis=1, keepdims=True), (plane * cap, LANES))
            stage_cot[src, :, :, width:] = gate.astype(BF).reshape(plane, cap, LANES)

        def part(c, carry):
            cols = pl.ds(pl.multiple_of(c * step, step), step)
            rows = sources[t][:, cols] if own else line[t, src, :, cols]
            put = jnp.dot(mark, rows, preferred_element_type=F32).astype(BF)
            stages[t][src, :, :, cols] = put.reshape(plane, cap, step)
            return carry

        lax.fori_loop(0, width // step, part, 0)
        own_copy(t, src).start()

        def push(q, carry):
            plane_copy(t, src, q).start()
            return carry

        lax.fori_loop(1, plane, push, 0)

    can_go = (o < outer - 1, o > 0)
    for kind in (2, 0, 1):
        for way in range(2):

            @pl.when(can_go[way])
            def _():
                hop(kind, o, way, True).start()

    for t in range(2):
        place(t, o, True)
    table_out(o, True).start()

    for j in range(1, outer):
        for way in range(2):
            src = o - j if way == 0 else o + j
            here = src >= 0 if way == 0 else src < outer

            @pl.when(here)
            def _():
                for kind in (2, 0, 1):
                    hop(kind, src, way, False).wait_recv()

                    @pl.when(can_go[way])
                    def _():
                        hop(kind, src, way, False).start()

                    if kind < 2:
                        place(kind, src, False)
                table_out(src, False).start()

    for kind in (2, 0, 1):
        for way in range(2):

            @pl.when(can_go[way])
            def _():
                hop(kind, o, way, True).wait_send()

                for j in range(1, outer):
                    src = o - j if way == 0 else o + j
                    here = src >= 0 if way == 0 else src < outer

                    @pl.when(here)
                    def _():
                        hop(kind, src, way, False).wait_send()

    table_out(o, True).wait()
    for j in range(1, outer):
        for way in range(2):
            src = o - j if way == 0 else o + j
            here = src >= 0 if way == 0 else src < outer

            @pl.when(here)
            def _():
                table_out(src, False).wait()

    for t in range(2):
        for src in range(outer):
            own_copy(t, src).wait()

            def finish(q, carry):
                plane_copy(t, src, q).wait_recv()
                plane_copy(t, src, q).wait_send()
                return carry

            lax.fori_loop(1, plane, finish, 0)


def dispatch(normed, cot, table, seqs, outer, inner, cap):
    rows, width = normed.shape
    plane = seqs * inner
    count = plane * outer
    vmem = pl.BlockSpec(memory_space=pltpu.VMEM)
    anywhere = pl.BlockSpec(memory_space=pl.ANY)
    dma = pltpu.SemaphoreType.DMA
    return pl.pallas_call(
        functools.partial(dispatch_kernel, seqs, outer, inner),
        out_shape=(
            jax.ShapeDtypeStruct((count, cap, width), BF),
            jax.ShapeDtypeStruct((count, cap, width + LANES), BF),
            jax.ShapeDtypeStruct(table.shape, BF),
        ),
        in_specs=[vmem, vmem, vmem],
        out_specs=(anywhere, anywhere, anywhere),
        scratch_shapes=[
            pltpu.VMEM((2, outer, rows, width), BF),
            pltpu.VMEM((outer,) + table.shape, BF),
            pltpu.VMEM((outer, plane, cap, width + LANES), BF),
            pltpu.VMEM((outer, plane, cap, width), BF),
            dma((2, outer, 2)),
            dma((2, outer)),
            dma((outer, 2)),
            dma((outer,)),
            dma((2, outer, plane)),
            dma((2, outer, plane)),
            dma((2, outer)),
            dma((outer,)),
        ],
        compiler_params=pltpu.CompilerParams(
            collective_id=0, has_side_effects=True, vmem_limit_bytes=40 * 1024 * 1024
        ),
        name="dispatch",
    )(normed, cot, table)


def expert_backward(rows_in, rows_cot, rows_gate, gate_w, up_w, down_w):
    pre_gate = jnp.dot(rows_in, gate_w, preferred_element_type=F32)
    pre_up = jnp.dot(rows_in, up_w, preferred_element_type=F32)
    sigmoid_gate = jax.nn.sigmoid(pre_gate)
    silu_gate = pre_gate * sigmoid_gate
    act = (silu_gate * pre_up).astype(BF)
    expert_out = jnp.dot(act, down_w, preferred_element_type=F32)
    slot_grad = jnp.sum(rows_cot.astype(F32) * expert_out, axis=1).astype(BF)
    d_expert = (rows_gate.astype(F32)[:, None] * rows_cot.astype(F32)).astype(BF)
    d_act = lax.dot_general(d_expert, down_w, (((1,), (1,)), ((), ())), preferred_element_type=F32)
    grad_gate = (d_act * pre_up * sigmoid_gate * (1.0 + pre_gate * (1.0 - sigmoid_gate))).astype(BF)
    grad_up = (d_act * silu_gate).astype(BF)
    turned = (((0,), (0,)), ((), ()))
    grad_down_w = lax.dot_general(act, d_expert, turned, preferred_element_type=F32).astype(BF)
    grad_gate_w = lax.dot_general(rows_in, grad_gate, turned, preferred_element_type=F32).astype(BF)
    grad_up_w = lax.dot_general(rows_in, grad_up, turned, preferred_element_type=F32).astype(BF)
    across = (((1,), (1,)), ((), ()))
    d_rows = (
        lax.dot_general(grad_gate, gate_w, across, preferred_element_type=F32)
        + lax.dot_general(grad_up, up_w, across, preferred_element_type=F32)
    ).astype(BF)
    return (d_rows, slot_grad, grad_gate_w, grad_up_w, grad_down_w)


def body(hidden_in, d_output, gain, route_ids, gates, w_gate, w_up, w_down):
    tok_rows, width = hidden_in.shape
    top_count = route_ids.shape[1]
    seqs = lax.axis_size("seq")
    per_seq = lax.axis_size("expert")
    outer = 4 if per_seq % 4 == 0 else 2
    inner = per_seq // outer
    devices = seqs * per_seq
    experts = w_gate.shape[0] * devices
    capacity = max(2, tok_rows * top_count * 3 // (2 * experts))
    cap = -(-capacity // 8) * 8
    wide_rows = hidden_in.astype(F32)
    inverse_rms = lax.rsqrt(jnp.mean(wide_rows * wide_rows, axis=1, keepdims=True) + 1e-06)
    unit_rows = wide_rows * inverse_rms
    normed = (unit_rows * gain[None, :]).astype(BF)

    ids_t = route_ids.T
    gates_t = gates.T
    names = jnp.arange(experts, dtype=jnp.int32)
    hit = ids_t[:, None, :] == names[None, :, None]
    chosen = jnp.any(hit, axis=0)
    gate_map = jnp.sum(jnp.where(hit, gates_t[:, None, :].astype(F32), 0.0), axis=0)
    token = jnp.arange(tok_rows, dtype=jnp.int32)
    earlier = (token[:, None] < token[None, :]).astype(BF)
    position = jnp.dot(chosen.astype(BF), earlier, preferred_element_type=F32).astype(jnp.int32)
    placed = chosen[:, None, :] & (position[:, None, :] == jnp.arange(cap, dtype=jnp.int32)[None, :, None])
    table = placed.astype(BF)
    gate_table = jnp.where(placed, gate_map[:, None, :], 0.0).astype(BF)
    by_plane = (
        gate_table.reshape(seqs, outer, inner, cap, tok_rows)
        .transpose(1, 0, 2, 3, 4)
        .reshape(outer, seqs * inner * cap, tok_rows)
    )
    got_in, got_cot, _ = dispatch(normed, d_output, by_plane, seqs, outer, inner, cap)
    d_rows, slot_grad, grad_gate_w, grad_up_w, grad_down_w = expert_backward(
        got_in.reshape(-1, width), got_cot[:, :, :width].reshape(-1, width),
        got_cot[:, :, width].reshape(-1),
        w_gate[0], w_up[0], w_down[0],
    )
    back = jnp.concatenate(
        [d_rows, jnp.broadcast_to(slot_grad[:, None], (slot_grad.shape[0], LANES))], axis=1
    ).reshape(devices, cap, width + LANES)
    home = lax.all_to_all(back, AXES, split_axis=0, concat_axis=0, tiled=True)
    home_rows = home[:, :, :width]
    home_grad = home[:, :, width]
    d_normed = lax.dot_general(
        table.reshape(-1, tok_rows), home_rows.reshape(-1, width), (((0,), (0,)), ((), ())),
        preferred_element_type=F32,
    )
    grad_map = jnp.sum(jnp.where(placed, home_grad[:, :, None].astype(F32), 0.0), axis=1)
    d_gates = jnp.sum(jnp.where(hit, grad_map[None], 0.0), axis=1).astype(BF).T
    gain_term = jnp.sum(d_normed * unit_rows, axis=0)
    gain_parts = lax.all_to_all(
        gain_term.reshape(devices, -1), AXES, split_axis=0, concat_axis=0, tiled=True
    )
    d_gain = jnp.sum(gain_parts, axis=0)
    d_unit = d_normed * gain[None, :]
    inner_mean = jnp.mean(d_unit * unit_rows, axis=1, keepdims=True)
    d_hidden_in = (
        d_output.astype(F32) + inverse_rms * (d_unit - unit_rows * inner_mean)
    ).astype(BF)
    return (d_hidden_in, d_gain, d_gates, grad_gate_w[None], grad_up_w[None], grad_down_w[None])


def solution(mesh):
    rows = P(AXES, None)
    blocks = P(AXES, None, None)
    return jax.shard_map(
        body,
        mesh=mesh,
        in_specs=(rows, rows, P(), rows, rows, blocks, blocks, blocks),
        out_specs=(rows, P(AXES), rows, blocks, blocks, blocks),
        check_vma=False,
    )
```

time: 279 us -> 235 us (0.84)
  starting transfers between devices: 31.6 us -> 6.2 us
  Pallas kernels: 108 us -> 99.1 us
  blocking collectives: 8.84 us -> 0 us
  local copies, waits for them, and re-layouts: 5.49 us -> 13.9 us
  matrix products: 45.3 us -> 37.3 us
  waiting for transfers between devices: 67.4 us -> 63.7 us
    all_to_all x2 -> x1, starting transfers between devices: 29 us -> 3.65 us  [body(): home = lax.all_to_all(back, AXES, split_axis=0, concat_axis=0, tiled=True)]
    all_to_all x1 -> x0, blocking collectives: 8.84 us -> none  [body(): lax.all_to_all(send_gate, AXES, split_axis=0, concat_axis=0, tiled=True)]
    pallas_call x1, Pallas kernels: 108 us -> 99.1 us  [dispatch(): pl.pallas_call(functools.partial(dispatch_kernel, seqs, outer, inner), ou...]
    slice x0 -> x3, local copies, waits for them, and re-layouts: none -> 5.4 us  [the longest x1 2.35 us: body(): home_rows = home[:, :, :width]]
    unnamed x38 -> x51, local copies, waits for them, and re-layouts: 3.76 us -> 7.22 us
    all_to_all x2 -> x1, waiting for transfers between devices: 63 us -> 59.9 us  [body(): home = lax.all_to_all(back, AXES, split_axis=0, concat_axis=0, tiled=True)]
  transfers between devices with their start and end apart: 3 -> 2, of which waited for: 3 -> 2; matrix products, arithmetic and copies ran while one was open for 7% -> 8% of each run, Pallas kernels for 0% -> 0%
where the time goes in v2:
time: 235 us
  Pallas kernels  99.1 us (42%)
  waiting for transfers between devices  63.7 us (27%)
  matrix products  37.3 us (16%)
  local copies, waits for them, and re-layouts  13.9 us (6%)
  other arithmetic  13.3 us (6%)
  starting transfers between devices  6.2 us (3%)
    pallas_call x1, Pallas kernels, dispatch(): pl.pallas_call(functools.partial(dispatch_kernel, seqs, outer, inner), ou...  99.1 us
    all_to_all x1, waiting for transfers between devices, body(): home = lax.all_to_all(back, AXES, split_axis=0, concat_axis=0, tiled=True)  59.9 us
    unnamed x51, local copies, waits for them, and re-layouts  7.22 us
    dot_general x1, matrix products, expert_backward(): lax.dot_general(rows_in, grad_up, turned, preferred_element_type=F32)  6.71 us
  transfers between devices with their start and end apart: 2, of which 2 were waited for; matrix products, arithmetic and copies ran while one was open for 8% of the time, Pallas kernels for 0%

profile of v2, /device:TPU:0, one launch (start us, length us, event | category | flops | bytes accessed | tf_op | source)
XLA Modules:
  0.0 234.5 jit_solution(13246190414850300304)
XLA Ops:
  0.6 0.8 fusion.41
  1.7 1.2 fusion.33
  2.9 0.7 convert_bitcast_fusion
  3.7 0.7 select_reduce_fusion.2
  4.4 1.2 fusion.26.normed
  5.8 1.0 copy-done.4
  6.8 99.1 %dispatch.1 = (bf16[32,24,2048]{2,1,0:T(8,128)(2,1)S(1)}, bf16[32,24,2176]{2,1,0:T(8,128)(2,1)S(1)}, bf16[4,192,128]{2,1,0:T(8,128)(2,1)}) custom-call(bf16[128,2048]{1,0:T(8,128)(2,1)S(1)} %fusion.26.normed, bf16[128,2048]{1,0:T(8,128)(2,1)S(1)} %copy-done.4, bf16[4,192,128]{2,1,0:T(8,128)(2,1)S(1)} %fusion.34.table), custom_call_target="tpu_custom_call" | custom-call | tf_op jit(solution)/shard_map/dispatch/pallas_call | solution.py:196
  106.0 1.7 copy-done.5
  107.7 1.7 copy-done.1
  109.4 2.1 slice.13
  111.7 4.6 %fusion.7 = f32[768,768]{1,0:T(8,128)S(1)} fusion(bf16[768,2048]{1,0:T(8,128)(2,1)} %bitcast.82, bf16[1,2048,768]{2,1,0:T(8,128)(2,1)S(1)} %copy-done), kind=kOutput, calls=%fused_computation.15 | convolution fusion | flops 2415919104 | bytes 8650752 | tf_op jit(solution)/shard_map/dot_general | solution.py:227
  116.4 2.6 %fusion.10 = f32[768,768]{1,0:T(8,128)S(1)} fusion(bf16[768,2048]{1,0:T(8,128)(2,1)S(1)} %bitcast.84, bf16[1,2048,768]{2,1,0:T(8,128)(2,1)S(1)} %copy-done.19), kind=kOutput, calls=%fused_computation.18 | convolution fusion | flops 2415919104 | bytes 8650752 | tf_op jit(solution)/shard_map/dot_general | solution.py:228
  119.6 1.3 copy-done.18
  120.9 3.5 %multiply_convert_fusion.1 = (bf16[768,768]{1,0:T(8,128)(2,1)S(1)}, bf16[768,768]{1,0:T(8,128)(2,1)S(1)}, bf16[768,768]{1,0:T(8,128)(2,1)S(1)}) fusion(f32[768,768]{1,0:T(8,128)S(1)} %fusion.7, f32[768,768]{1,0:T(8,128)S(1)} %fusion.10, bf16[768,2048]{1,0:T(8,128)(2,1)S(1)} %bitcast.87, bf16[1,768,2048]{2,1,0:T(8,128)(2,1)S(1)} %copy-done.18), kind=kOutput, calls=%fused_computation.28 | convolution fusion | flops 2424766464 | bytes 14548992 | tf_op jit(solution)/shard_map/dot_general | solution.py:235
  124.4 2.6 %fusion.5 = f32[768,2048]{1,0:T(8,128)S(1)} fusion(bf16[768,768]{1,0:T(8,128)(2,1)S(1)} %get-tuple-element.13, bf16[1,2048,768]{2,1,0:T(8,128)(2,1)S(1)} %copy-done), kind=kOutput, calls=%fused_computation.13 | convolution fusion | flops 2415919104 | bytes 10616832 | tf_op jit(solution)/shard_map/dot_general | solution.py:244
  127.6 3.0 %fusion.1 = bf16[768]{0:T(1024)(128)(2,1)S(1)} fusion(bf16[32,24,2048]{2,1,0:T(8,128)(2,1)S(1)} %copy-done.9, bf16[768,768]{1,0:T(8,128)(2,1)S(1)} %get-tuple-element.14, bf16[1,768,2048]{2,1,0:T(8,128)(2,1)S(1)} %copy-done.18), kind=kOutput, calls=%fused_computation.4 | convolution fusion | flops 2420636928 | bytes 7472640 | tf_op jit(solution)/shard_map/dot_general | solution.py:232
  130.6 3.1 %add_convert_fusion = bf16[768,2048]{1,0:T(8,128)(2,1)S(1)} fusion(f32[768,2048]{1,0:T(8,128)S(1)} %fusion.5, bf16[768,768]{1,0:T(8,128)(2,1)S(1)} %get-tuple-element.12, bf16[1,2048,768]{2,1,0:T(8,128)(2,1)S(1)} %copy-done.19), kind=kOutput, calls=%fused_computation.6 | convolution fusion | flops 2419064832 | bytes 13762560 | tf_op jit(solution)/shard_map/dot_general | solution.py:245
  133.8 2.1 pad_maximum_fusion
  135.9 3.6 %all-to-all-start = ((bf16[32,24,2176]{2,1,0:T(8,128)(2,1)}), bf16[32,24,2176]{2,1,0:T(8,128)(2,1)}, u32[]{:S(2)}, u32[]{:S(2)}) async-start(bf16[32,24,2176]{2,1,0:T(8,128)(2,1)} %bitcast.86), calls=%async_computation | async-start | bytes 6684672 | tf_op jit(solution)/shard_map/all_to_all | solution.py:292
  139.6 1.1 fusion.40
  140.8 6.7 %fusion.16 = bf16[1,2048,768]{2,1,0:T(8,128)(2,1)} fusion(bf16[768,2048]{1,0:T(8,128)(2,1)} %bitcast.83, bf16[768,768]{1,0:T(8,128)(2,1)} %copy-done.24), kind=kOutput, calls=%fused_computation.24 | convolution fusion | flops 2417491968 | bytes 7471104 | tf_op jit(solution)/shard_map/dot_general | solution.py:241
  147.5 4.1 %fusion.15 = bf16[1,2048,768]{2,1,0:T(8,128)(2,1)} fusion(bf16[768,2048]{1,0:T(8,128)(2,1)S(1)} %bitcast.85, bf16[768,768]{1,0:T(8,128)(2,1)S(1)} %copy-done.21), kind=kOutput, calls=%fused_computation.23 | convolution fusion | flops 2417491968 | bytes 7471104 | tf_op jit(solution)/shard_map/dot_general | solution.py:240
  152.2 0.7 copy-done.23
  152.9 4.0 %fusion.17 = bf16[1,768,2048]{2,1,0:T(8,128)(2,1)} fusion(bf16[768,768]{1,0:T(8,128)(2,1)S(1)} %copy-done.23, bf16[768,2048]{1,0:T(8,128)(2,1)S(1)} %fusion.2), kind=kOutput, calls=%fused_computation.25 | convolution fusion | flops 2417491968 | bytes 7471104 | tf_op jit(solution)/shard_map/dot_general | solution.py:239
  156.9 59.9 %all-to-all-done = bf16[32,24,2176]{2,1,0:T(8,128)(2,1)} async-done(((bf16[32,24,2176]{2,1,0:T(8,128)(2,1)}), bf16[32,24,2176]{2,1,0:T(8,128)(2,1)}, u32[]{:S(2)}, u32[]{:S(2)}) %all-to-all-start) | async-done | bytes 3342368 | tf_op jit(solution)/shard_map/all_to_all | solution.py:292
  216.8 2.3 %slice.16 = bf16[32,24,2048]{2,1,0:T(8,128)(2,1)S(1)} slice(bf16[32,24,2176]{2,1,0:T(8,128)(2,1)} %all-to-all-done), slice={[0:32], [0:24], [0:2048]} | slice | bytes 6291456 | tf_op jit(solution)/shard_map/slice | solution.py:293
  219.2 3.0 %fusion.32 = (f32[2048]{0:T(1024)S(1)}, f32[128]{0:T(128)S(1)}, f32[128,2048]{1,0:T(8,128)}) fusion(bf16[128,2048]{1,0:T(8,128)(2,1)S(1)} %copy-done.8, f32[128]{0:T(128)S(1)} %copy-done.17, f32[2048]{0:T(1024)S(1)} %copy-done.14, bf16[32,24,2048]{2,1,0:T(8,128)(2,1)S(1)} %slice.16, s32[32,128]{1,0:T(8,128)S(1)} %copy-done.11, ...), kind=kOutput, calls=%fused_computation.45 | convolution fusion | flops 404682624 | bytes 4756480 | tf_op jit(solution)/shard_map/dot_general | solution.py:295
  222.2 1.0 slice.17
  223.6 0.7 all_to_all.10
  224.3 2.6 %all-to-all-start.1 = ((f32[32,1,64]{2,1,0:T(1,128)}), f32[32,1,64]{2,1,0:T(1,128)S(1)}, u32[]{:S(2)}, u32[]{:S(2)}) async-start(f32[32,1,64]{2,1,0:T(1,128)} %all_to_all.10), calls=%async_computation.1 | async-start | bytes 32768 | tf_op jit(solution)/shard_map/all_to_all | solution.py:302
  226.9 2.7 %fusion.31 = bf16[128,2048]{1,0:T(8,128)(2,1)} fusion(bf16[128,2048]{1,0:T(8,128)(2,1)} %param.8, bf16[128,2048]{1,0:T(8,128)(2,1)} %cot.1, f32[128,2048]{1,0:T(8,128)} %get-tuple-element.15, f32[128]{0:T(128)S(1)} %broadcast_multiply_fusion, f32[2048]{0:T(1024)S(1)} %copy-done.14, f32[128]{0:T(128)S(1)} %copy-done.17), kind=kLoop, calls=%fused_computation.44 | loop fusion | flops 2359296 | bytes 2630656 | tf_op jit(solution)/shard_map/convert_element_type | solution.py:310
  230.2 3.8 %all-to-all-done.1 = f32[32,1,64]{2,1,0:T(1,128)S(1)} async-done(((f32[32,1,64]{2,1,0:T(1,128)}), f32[32,1,64]{2,1,0:T(1,128)S(1)}, u32[]{:S(2)}, u32[]{:S(2)}) %all-to-all-start.1) | async-done | bytes 8224 | tf_op jit(solution)/shard_map/all_to_all | solution.py:302
  (63 shorter events, 4.2 us)
Async XLA Ops:
  0.6 111.1 %copy-start = (bf16[1,2048,768]{2,1,0:T(8,128)(2,1)S(1)}, bf16[1,2048,768]{2,1,0:T(8,128)(2,1)}, u32[]{:S(2)}) copy-start(bf16[1,2048,768]{2,1,0:T(8,128)(2,1)} %param.13) | copy-start | bytes 9437188
  1.5 104.4 %copy-start.12 = (pred[32,128]{1,0:T(8,128)(4,1)}, pred[32,128]{1,0:T(8,128)(4,1)S(1)}, u32[]{:S(2)}) copy-start(pred[32,128]{1,0:T(8,128)(4,1)S(1)} %fusion.41) | copy-start | bytes 12292
  1.7 104.3 %copy-start.10 = (s32[32,128]{1,0:T(8,128)}, s32[32,128]{1,0:T(8,128)S(1)}, u32[]{:S(2)}) copy-start(s32[32,128]{1,0:T(8,128)S(1)} %convolution_convert_fusion.3) | copy-start | bytes 49156
  2.9 103.0 %copy-start.16 = (f32[128]{0:T(128)}, f32[128]{0:T(128)S(1)}, u32[]{:S(2)}) copy-start(f32[128]{0:T(128)S(1)} %add_rsqrt_fusion) | copy-start | bytes 1540
  5.8 1.0 copy-start.4
  106.0 1.7 copy-start.5
  107.6 1.7 copy-start.1
  111.7 4.7 %copy-start.6 = (bf16[32,24,2048]{2,1,0:T(8,128)(2,1)S(1)}, bf16[32,24,2048]{2,1,0:T(8,128)(2,1)}, u32[]{:S(2)}) copy-start(bf16[32,24,2048]{2,1,0:T(8,128)(2,1)} %copy-done.5) | copy-start | bytes 9437188
  111.7 4.7 %copy-start.19 = (bf16[1,2048,768]{2,1,0:T(8,128)(2,1)S(1)}, bf16[1,2048,768]{2,1,0:T(8,128)(2,1)}, u32[]{:S(2)}) copy-start(bf16[1,2048,768]{2,1,0:T(8,128)(2,1)} %param.14) | copy-start | bytes 9437188
  116.4 2.6 %copy-start.2 = (bf16[32,24,2176]{2,1,0:T(8,128)(2,1)S(1)}, bf16[32,24,2176]{2,1,0:T(8,128)(2,1)}, u32[]{:S(2)}) copy-start(bf16[32,24,2176]{2,1,0:T(8,128)(2,1)} %copy-done.1) | copy-start | bytes 10027012
  119.0 1.9 copy-start.18
  124.4 2.7 %copy-start.20 = (bf16[768,768]{1,0:T(8,128)(2,1)}, bf16[768,768]{1,0:T(8,128)(2,1)S(1)}, u32[]{:S(2)}) copy-start(bf16[768,768]{1,0:T(8,128)(2,1)S(1)} %get-tuple-element.13) | copy-start | bytes 3538948
  124.4 2.7 %copy-start.22 = (bf16[768,768]{1,0:T(8,128)(2,1)}, bf16[768,768]{1,0:T(8,128)(2,1)S(1)}, u32[]{:S(2)}) copy-start(bf16[768,768]{1,0:T(8,128)(2,1)S(1)} %get-tuple-element.14) | copy-start | bytes 3538948
  124.4 6.2 %copy-start.24 = (bf16[768,768]{1,0:T(8,128)(2,1)}, bf16[768,768]{1,0:T(8,128)(2,1)S(1)}, u32[]{:S(2)}) copy-start(bf16[768,768]{1,0:T(8,128)(2,1)S(1)} %get-tuple-element.12) | copy-start | bytes 3538948
  124.4 3.2 %copy-start.9 = (bf16[32,24,2048]{2,1,0:T(8,128)(2,1)S(1)}, bf16[32,24,2048]{2,1,0:T(8,128)(2,1)}, u32[]{:S(2)}) copy-start(bf16[32,24,2048]{2,1,0:T(8,128)(2,1)} %slice.13) | copy-start | bytes 9437188
  135.9 80.9 %all-to-all-start = ((bf16[32,24,2176]{2,1,0:T(8,128)(2,1)}), bf16[32,24,2176]{2,1,0:T(8,128)(2,1)}, u32[]{:S(2)}, u32[]{:S(2)}) async-start(bf16[32,24,2176]{2,1,0:T(8,128)(2,1)} %bitcast.86), calls=%async_computation | async-start | bytes 6684672 | tf_op jit(solution)/shard_map/all_to_all | solution.py:292
  140.8 6.7 %copy-start.7 = (bf16[32,24,2048]{2,1,0:T(8,128)(2,1)S(1)}, bf16[32,24,2048]{2,1,0:T(8,128)(2,1)}, u32[]{:S(2)}) copy-start(bf16[32,24,2048]{2,1,0:T(8,128)(2,1)} %copy-done.5) | copy-start | bytes 9437188
  140.8 6.7 %copy-start.21 = (bf16[768,768]{1,0:T(8,128)(2,1)S(1)}, bf16[768,768]{1,0:T(8,128)(2,1)}, u32[]{:S(2)}) copy-start(bf16[768,768]{1,0:T(8,128)(2,1)} %copy-done.20) | copy-start | bytes 3538948
  147.5 4.1 %copy-start.3 = (bf16[32,24,2176]{2,1,0:T(8,128)(2,1)S(1)}, bf16[32,24,2176]{2,1,0:T(8,128)(2,1)}, u32[]{:S(2)}) copy-start(bf16[32,24,2176]{2,1,0:T(8,128)(2,1)} %copy-done.1) | copy-start | bytes 10027012
  151.6 1.3 copy-start.23
  156.9 62.3 %copy-start.11 = (s32[32,128]{1,0:T(8,128)S(1)}, s32[32,128]{1,0:T(8,128)}, u32[]{:S(2)}) copy-start(s32[32,128]{1,0:T(8,128)} %copy-done.10) | copy-start | bytes 49156
  156.9 62.3 %copy-start.13 = (pred[32,128]{1,0:T(8,128)(4,1)S(1)}, pred[32,128]{1,0:T(8,128)(4,1)}, u32[]{:S(2)}) copy-start(pred[32,128]{1,0:T(8,128)(4,1)} %copy-done.12) | copy-start | bytes 12292
  156.9 62.3 %copy-start.14 = (f32[2048]{0:T(1024)S(1)}, f32[2048]{0:T(1024)}, u32[]{:S(2)}) copy-start(f32[2048]{0:T(1024)} %param.10) | copy-start | bytes 24580
  156.9 62.3 %copy-start.17 = (f32[128]{0:T(128)S(1)}, f32[128]{0:T(128)}, u32[]{:S(2)}) copy-start(f32[128]{0:T(128)} %copy-done.16) | copy-start | bytes 1540
  216.8 2.4 %copy-start.8 = (bf16[128,2048]{1,0:T(8,128)(2,1)S(1)}, bf16[128,2048]{1,0:T(8,128)(2,1)}, u32[]{:S(2)}) copy-start(bf16[128,2048]{1,0:T(8,128)(2,1)} %param.8) | copy-start | bytes 1572868
  222.2 7.4 %copy-start.15 = (s32[128,4]{0,1:T(4,128)S(1)}, s32[128,4]{0,1:T(4,128)}, u32[]{:S(2)}) copy-start(s32[128,4]{0,1:T(4,128)} %param.11) | copy-start | bytes 6148
  224.3 9.7 %all-to-all-start.1 = ((f32[32,1,64]{2,1,0:T(1,128)}), f32[32,1,64]{2,1,0:T(1,128)S(1)}, u32[]{:S(2)}, u32[]{:S(2)}) async-start(f32[32,1,64]{2,1,0:T(1,128)} %all_to_all.10), calls=%async_computation.1 | async-start | bytes 32768 | tf_op jit(solution)/shard_map/all_to_all | solution.py:302

commit v3 on v2

--- a/solution.py
+++ b/solution.py
@@ -223,6 +223,186 @@
     )(normed, cot, table)
 
 
+def collect_kernel(
+    seqs, outer, inner, back, table, out_rows, out_grad,
+    landed, running, stage, plane_send, plane_recv, own_sem, run_send, run_recv,
+):
+    s, o, i = coords(outer, inner)
+    plane = seqs * inner
+    p = s * inner + i
+    cap = landed.shape[2]
+    wide = landed.shape[3]
+    width = wide - LANES
+    greet_all(s, o, i, seqs, outer, inner)
+
+    def plane_copy(src, q):
+        to = (p + q) % plane
+        home = (to // inner) * (outer * inner) + src * inner + to % inner
+        return remote(
+            back.at[home], landed.at[src, p], plane_send.at[src, q], plane_recv.at[src, q],
+            (to // inner, o * inner + to % inner),
+        )
+
+    def own_copy(src):
+        home = s * (outer * inner) + src * inner + i
+        return pltpu.make_async_copy(back.at[home], landed.at[src, p], own_sem.at[src])
+
+    def run_copy(src, way):
+        peer = (s, (o - 1 + 2 * way) * inner + i)
+        return remote(
+            stage.at[src], running.at[src, way], run_send.at[src, way], run_recv.at[src, way], peer
+        )
+
+    def cases(j):
+        return ((o - j, o - j >= 0, 0), (o + j, o + j < outer, 1))
+
+    def push_all(src):
+        own_copy(src).start()
+
+        def push(q, carry):
+            plane_copy(src, q).start()
+            return carry
+
+        lax.fori_loop(1, plane, push, 0)
+
+    def await_all(src):
+        own_copy(src).wait()
+
+        def wait(q, carry):
+            plane_copy(src, q).wait_recv()
+            return carry
+
+        lax.fori_loop(1, plane, wait, 0)
+
+    turned = (((0,), (0,)), ((), ()))
+
+    def marks(src):
+        return jnp.where(table[src].astype(F32) != 0.0, 1.0, 0.0).astype(BF)
+
+    def sums(src, cols, size):
+        values = landed[src, :, :, cols].reshape(plane * cap, size)
+        return lax.dot_general(marks(src), values, turned, preferred_element_type=F32)
+
+    def grads(src):
+        values = landed[src, :, :, width:].astype(F32)
+        column = lax.broadcasted_iota(jnp.int32, values.shape, 2)
+        expert = o * plane + lax.broadcasted_iota(jnp.int32, values.shape, 0)
+        values = jnp.where(column == expert, values, 0.0).reshape(plane * cap, LANES).astype(BF)
+        return lax.dot_general(marks(src), values, turned, preferred_element_type=F32)
+
+    step = 512 if width % 512 == 0 else width
+
+    def each(part):
+        def one(c, carry):
+            part(pl.ds(pl.multiple_of(c * step, step), step))
+            return carry
+
+        lax.fori_loop(0, width // step, one, 0)
+
+    for j in range(outer - 1, 0, -1):
+        for src, here, way in cases(j):
+
+            @pl.when(here)
+            def _():
+                push_all(src)
+
+    push_all(o)
+
+    more = (o < outer - 1, o > 0)
+    for j in range(outer - 1, 0, -1):
+        for src, here, way in cases(j):
+
+            @pl.when(here)
+            def _():
+                await_all(src)
+
+                def first(cols):
+                    stage[src, :, cols] = sums(src, cols, step).astype(BF)
+
+                def later(cols):
+                    total = sums(src, cols, step) + running[src, way, :, cols].astype(F32)
+                    stage[src, :, cols] = total.astype(BF)
+
+                @pl.when(more[way])
+                def _():
+                    run_copy(src, way).wait_recv()
+                    each(later)
+                    total = grads(src) + running[src, way, :, width:].astype(F32)
+                    stage[src, :, width:] = total.astype(BF)
+
+                @pl.when(jnp.logical_not(more[way]))
+                def _():
+                    each(first)
+                    stage[src, :, width:] = grads(src).astype(BF)
+
+                run_copy(src, way).start()
+
+    await_all(o)
+
+    def mine(cols):
+        out_rows[:, cols] = sums(o, cols, step)
+
+    each(mine)
+    out_grad[...] = grads(o)
+    for way in range(2):
+
+        @pl.when(more[way])
+        def _():
+            run_copy(o, way).wait_recv()
+
+            def add(cols):
+                out_rows[:, cols] = out_rows[:, cols] + running[o, way, :, cols].astype(F32)
+
+            each(add)
+            out_grad[...] = out_grad[...] + running[o, way, :, width:].astype(F32)
+
+    for j in range(1, outer):
+        for src, here, way in cases(j):
+
+            @pl.when(here)
+            def _():
+                run_copy(src, way).wait_send()
+
+    for src in range(outer):
+
+        def finish(q, carry):
+            plane_copy(src, q).wait_send()
+            return carry
+
+        lax.fori_loop(1, plane, finish, 0)
+
+
+def collect(back, table, seqs, outer, inner):
+    count, cap, wide = back.shape
+    plane = seqs * inner
+    rows = table.shape[2]
+    vmem = pl.BlockSpec(memory_space=pltpu.VMEM)
+    dma = pltpu.SemaphoreType.DMA
+    return pl.pallas_call(
+        functools.partial(collect_kernel, seqs, outer, inner),
+        out_shape=(
+            jax.ShapeDtypeStruct((rows, wide - LANES), F32),
+            jax.ShapeDtypeStruct((rows, LANES), F32),
+        ),
+        in_specs=[pl.BlockSpec(memory_space=pl.ANY), vmem],
+        out_specs=(vmem, vmem),
+        scratch_shapes=[
+            pltpu.VMEM((outer, plane, cap, wide), BF),
+            pltpu.VMEM((outer, 2, rows, wide), BF),
+            pltpu.VMEM((outer, rows, wide), BF),
+            dma((outer, plane)),
+            dma((outer, plane)),
+            dma((outer,)),
+            dma((outer, 2)),
+            dma((outer, 2)),
+        ],
+        compiler_params=pltpu.CompilerParams(
+            collective_id=1, has_side_effects=True, vmem_limit_bytes=40 * 1024 * 1024
+        ),
+        name="collect",
+    )(back, table)
+
+
 def expert_backward(rows_in, rows_cot, rows_gate, gate_w, up_w, down_w):
     pre_gate = jnp.dot(rows_in, gate_w, preferred_element_type=F32)
     pre_up = jnp.dot(rows_in, up_w, preferred_element_type=F32)
@@ -280,7 +460,7 @@
         .transpose(1, 0, 2, 3, 4)
         .reshape(outer, seqs * inner * cap, tok_rows)
     )
-    got_in, got_cot, _ = dispatch(normed, d_output, by_plane, seqs, outer, inner, cap)
+    got_in, got_cot, tables = dispatch(normed, d_output, by_plane, seqs, outer, inner, cap)
     d_rows, slot_grad, grad_gate_w, grad_up_w, grad_down_w = expert_backward(
         got_in.reshape(-1, width), got_cot[:, :, :width].reshape(-1, width),
         got_cot[:, :, width].reshape(-1),
@@ -289,15 +469,14 @@
     back = jnp.concatenate(
         [d_rows, jnp.broadcast_to(slot_grad[:, None], (slot_grad.shape[0], LANES))], axis=1
     ).reshape(devices, cap, width + LANES)
-    home = lax.all_to_all(back, AXES, split_axis=0, concat_axis=0, tiled=True)
-    home_rows = home[:, :, :width]
-    home_grad = home[:, :, width]
-    d_normed = lax.dot_general(
-        table.reshape(-1, tok_rows), home_rows.reshape(-1, width), (((0,), (0,)), ((), ())),
-        preferred_element_type=F32,
+    d_normed, grad_map = collect(back, tables, seqs, outer, inner)
+    lane = jnp.arange(LANES, dtype=jnp.int32)
+    ids_column = (
+        route_ids // inner % outer * (seqs * inner) + route_ids // per_seq * inner + route_ids % inner
     )
-    grad_map = jnp.sum(jnp.where(placed, home_grad[:, :, None].astype(F32), 0.0), axis=1)
-    d_gates = jnp.sum(jnp.where(hit, grad_map[None], 0.0), axis=1).astype(BF).T
+    d_gates = jnp.sum(
+        jnp.where(ids_column[:, :, None] == lane[None, None, :], grad_map[:, None, :], 0.0), axis=2
+    ).astype(BF)
     gain_term = jnp.sum(d_normed * unit_rows, axis=0)
     gain_parts = lax.all_to_all(
         gain_term.reshape(devices, -1), AXES, split_axis=0, concat_axis=0, tiled=True

time: 235 us -> 218 us (0.928)
  waiting for transfers between devices: 63.7 us -> 0.01 us
  Pallas kernels: 99.1 us -> 151 us
  matrix products: 37.3 us -> 34.3 us
  local copies, waits for them, and re-layouts: 13.9 us -> 10.9 us
    all_to_all x1 -> x0, waiting for transfers between devices: 59.9 us -> none  [body(): home = lax.all_to_all(back, AXES, split_axis=0, concat_axis=0, tiled=True)]
    pallas_call x0 -> x1, Pallas kernels: none -> 51.9 us  [collect(): pl.pallas_call(functools.partial(collect_kernel, seqs, outer, inner), out...]
    all_to_all x1, starting transfers between devices: 2.55 us -> 7.2 us  [body(): lax.all_to_all(gain_term.reshape(devices, -1), AXES, split_axis=0, concat...]
    all_to_all x1, waiting for transfers between devices: 3.8 us -> 0.01 us  [body(): lax.all_to_all(gain_term.reshape(devices, -1), AXES, split_axis=0, concat...]
    all_to_all x1 -> x0, starting transfers between devices: 3.65 us -> none  [body(): home = lax.all_to_all(back, AXES, split_axis=0, concat_axis=0, tiled=True)]
    slice x2 -> x0, local copies, waits for them, and re-layouts: 3.31 us -> none  [the longest x1 2.35 us: body(): home_rows = home[:, :, :width]]
    dot_general x1 -> x0, matrix products: 2.99 us -> none  [body(): lax.dot_general(table.reshape(-1, tok_rows), home_rows.reshape(-1, width)...]
    unnamed x51 -> x44, local copies, waits for them, and re-layouts: 7.22 us -> 6.52 us
  transfers between devices with their start and end apart: 2 -> 1, of which waited for: 2 -> 0; matrix products, arithmetic and copies ran while one was open for 8% -> 9% of each run, Pallas kernels for 0% -> 0%
where the time goes in v3:
time: 218 us
  Pallas kernels  151 us (69%)
  matrix products  34.3 us (16%)
  other arithmetic  13.2 us (6%)
  local copies, waits for them, and re-layouts  10.9 us (5%)
  starting transfers between devices  7.2 us (3%)
    pallas_call x1, Pallas kernels, dispatch(): pl.pallas_call(functools.partial(dispatch_kernel, seqs, outer, inner), ou...  99.1 us
    pallas_call x1, Pallas kernels, collect(): pl.pallas_call(functools.partial(collect_kernel, seqs, outer, inner), out...  51.9 us
    all_to_all x1, starting transfers between devices, body(): lax.all_to_all(gain_term.reshape(devices, -1), AXES, split_axis=0, concat...  7.2 us
    dot_general x1, matrix products, expert_backward(): lax.dot_general(rows_in, grad_up, turned, preferred_element_type=F32)  6.71 us
    unnamed x44, local copies, waits for them, and re-layouts  6.52 us
    dot_general x1, matrix products, expert_backward(): pre_gate = jnp.dot(rows_in, gate_w, preferred_element_type=F32)  4.63 us
  transfers between devices with their start and end apart: 1, of which 0 were waited for; matrix products, arithmetic and copies ran while one was open for 9% of the time, Pallas kernels for 0%

profile of v3, /device:TPU:0, one launch (start us, length us, event | category | flops | bytes accessed | tf_op | source)
XLA Modules:
  0.0 217.6 jit_solution(7118123347467577849)
XLA Ops:
  0.6 0.8 fusion.32
  1.6 1.2 fusion.28
  2.9 0.7 convert_bitcast_fusion
  3.7 0.7 select_reduce_fusion.1
  4.4 1.2 fusion.21.normed
  5.8 1.0 copy-done.5
  6.8 99.1 %dispatch.1 = (bf16[32,24,2048]{2,1,0:T(8,128)(2,1)S(1)}, bf16[32,24,2176]{2,1,0:T(8,128)(2,1)S(1)}, bf16[4,192,128]{2,1,0:T(8,128)(2,1)S(1)}) custom-call(bf16[128,2048]{1,0:T(8,128)(2,1)S(1)} %fusion.21.normed, bf16[128,2048]{1,0:T(8,128)(2,1)S(1)} %copy-done.5, bf16[4,192,128]{2,1,0:T(8,128)(2,1)S(1)} %fusion.29.table), custom_call_target="tpu_custom_call" | custom-call | tf_op jit(solution)/shard_map/dispatch/pallas_call | solution.py:196
  106.0 1.7 copy-done.7
  107.6 0.8 slice_convert_fusion
  108.4 1.0 copy-done.1
  109.4 2.1 slice.7
  111.5 1.2 copy.33
  112.8 4.6 %fusion.5 = f32[768,768]{1,0:T(8,128)S(1)} fusion(bf16[768,2048]{1,0:T(8,128)(2,1)} %bitcast.75, bf16[1,2048,768]{2,1,0:T(8,128)(2,1)S(1)} %copy-done), kind=kOutput, calls=%fused_computation.13 | convolution fusion | flops 2415919104 | bytes 8650752 | tf_op jit(solution)/shard_map/dot_general | solution.py:407
  117.5 2.6 %fusion.8 = f32[768,768]{1,0:T(8,128)S(1)} fusion(bf16[768,2048]{1,0:T(8,128)(2,1)S(1)} %bitcast.77, bf16[1,2048,768]{2,1,0:T(8,128)(2,1)S(1)} %copy-done.16), kind=kOutput, calls=%fused_computation.16 | convolution fusion | flops 2415919104 | bytes 8650752 | tf_op jit(solution)/shard_map/dot_general | solution.py:408
  120.1 0.6 fusion
  120.7 1.3 copy-done.15
  122.0 3.4 %multiply_convert_fusion.1 = (bf16[768,768]{1,0:T(8,128)(2,1)S(1)}, bf16[768,768]{1,0:T(8,128)(2,1)S(1)}, bf16[768,768]{1,0:T(8,128)(2,1)S(1)}) fusion(f32[768,768]{1,0:T(8,128)S(1)} %fusion.5, f32[768,768]{1,0:T(8,128)S(1)} %fusion.8, bf16[768,2048]{1,0:T(8,128)(2,1)S(1)} %bitcast.79, bf16[1,768,2048]{2,1,0:T(8,128)(2,1)S(1)} %copy-done.15), kind=kOutput, calls=%fused_computation.25 | convolution fusion | flops 2424766464 | bytes 14548992 | tf_op jit(solution)/shard_map/dot_general | solution.py:415
  125.5 2.6 %fusion.3 = f32[768,2048]{1,0:T(8,128)S(1)} fusion(bf16[768,768]{1,0:T(8,128)(2,1)S(1)} %get-tuple-element.19, bf16[1,2048,768]{2,1,0:T(8,128)(2,1)S(1)} %copy-done), kind=kOutput, calls=%fused_computation.11 | convolution fusion | flops 2415919104 | bytes 10616832 | tf_op jit(solution)/shard_map/dot_general | solution.py:424
  128.6 3.0 %fusion.1 = bf16[768]{0:T(1024)(128)(2,1)S(1)} fusion(bf16[32,24,2048]{2,1,0:T(8,128)(2,1)S(1)} %copy-done.12, bf16[768,768]{1,0:T(8,128)(2,1)S(1)} %get-tuple-element.20, bf16[1,768,2048]{2,1,0:T(8,128)(2,1)S(1)} %copy-done.15), kind=kOutput, calls=%fused_computation.4 | convolution fusion | flops 2420636928 | bytes 7472640 | tf_op jit(solution)/shard_map/dot_general | solution.py:412
  131.6 3.1 %add_convert_fusion = bf16[768,2048]{1,0:T(8,128)(2,1)S(1)} fusion(f32[768,2048]{1,0:T(8,128)S(1)} %fusion.3, bf16[768,768]{1,0:T(8,128)(2,1)S(1)} %get-tuple-element.18, bf16[1,2048,768]{2,1,0:T(8,128)(2,1)S(1)} %copy-done.16), kind=kOutput, calls=%fused_computation.6 | convolution fusion | flops 2419064832 | bytes 13762560 | tf_op jit(solution)/shard_map/dot_general | solution.py:425
  135.2 51.9 %collect.1 = (f32[128,2048]{1,0:T(8,128)S(1)}, f32[128,128]{1,0:T(8,128)S(1)}) custom-call(bf16[32,24,2176]{2,1,0:T(8,128)(2,1)S(1)} %bitcast.74, bf16[4,192,128]{2,1,0:T(8,128)(2,1)S(1)} %get-tuple-element.13.table), custom_call_target="tpu_custom_call" | custom-call | tf_op jit(solution)/shard_map/collect/pallas_call | solution.py:381
  187.2 0.9 copy-done.3
  188.5 0.7 all_to_all.6
  189.2 7.2 %all-to-all-start = ((f32[32,1,64]{2,1,0:T(1,128)}), f32[32,1,64]{2,1,0:T(1,128)S(1)}, u32[]{:S(2)}, u32[]{:S(2)}) async-start(f32[32,1,64]{2,1,0:T(1,128)} %all_to_all.6), calls=%async_computation | async-start | bytes 32768 | tf_op jit(solution)/shard_map/all_to_all | solution.py:481
  196.4 1.1 fusion.31
  197.6 6.7 %fusion.14 = bf16[1,2048,768]{2,1,0:T(8,128)(2,1)} fusion(bf16[768,2048]{1,0:T(8,128)(2,1)} %bitcast.76, bf16[768,768]{1,0:T(8,128)(2,1)} %copy-done.21), kind=kOutput, calls=%fused_computation.22 | convolution fusion | flops 2417491968 | bytes 7471104 | tf_op jit(solution)/shard_map/dot_general | solution.py:421
  204.3 4.0 %fusion.13 = bf16[1,2048,768]{2,1,0:T(8,128)(2,1)} fusion(bf16[768,2048]{1,0:T(8,128)(2,1)S(1)} %bitcast.78, bf16[768,768]{1,0:T(8,128)(2,1)S(1)} %copy-done.18), kind=kOutput, calls=%fused_computation.21 | convolution fusion | flops 2417491968 | bytes 7471104 | tf_op jit(solution)/shard_map/dot_general | solution.py:420
  208.4 2.6 %fusion.2 = bf16[768,2048]{1,0:T(8,128)(2,1)S(1)} fusion(f32[768]{0:T(1024)S(1)} %reshape.81, bf16[32,24,2176]{2,1,0:T(8,128)(2,1)} %copy-done.1), kind=kLoop, calls=%fused_computation.5 | loop fusion | flops 4718592 | bytes 6294528 | tf_op jit(solution)/shard_map/convert_element_type | solution.py:414
  211.0 4.0 %fusion.15 = bf16[1,768,2048]{2,1,0:T(8,128)(2,1)} fusion(bf16[768,768]{1,0:T(8,128)(2,1)S(1)} %copy-done.20, bf16[768,2048]{1,0:T(8,128)(2,1)S(1)} %fusion.2), kind=kOutput, calls=%fused_computation.23 | convolution fusion | flops 2417491968 | bytes 7471104 | tf_op jit(solution)/shard_map/dot_general | solution.py:419
  215.1 1.2 fusion.26
  216.3 0.8 select_reduce_fusion
  217.1 0.5 reduce_sum.68
  (52 shorter events, 1.9 us)
Async XLA Ops:
  0.6 112.1 %copy-start = (bf16[1,2048,768]{2,1,0:T(8,128)(2,1)S(1)}, bf16[1,2048,768]{2,1,0:T(8,128)(2,1)}, u32[]{:S(2)}) copy-start(bf16[1,2048,768]{2,1,0:T(8,128)(2,1)} %param.13) | copy-start | bytes 9437188
  5.8 1.0 copy-start.5
  106.0 1.7 copy-start.7
  107.6 1.8 copy-start.1
  112.8 4.7 %copy-start.8 = (bf16[32,24,2048]{2,1,0:T(8,128)(2,1)S(1)}, bf16[32,24,2048]{2,1,0:T(8,128)(2,1)}, u32[]{:S(2)}) copy-start(bf16[32,24,2048]{2,1,0:T(8,128)(2,1)} %copy-done.7) | copy-start | bytes 9437188
  112.8 4.7 %copy-start.16 = (bf16[1,2048,768]{2,1,0:T(8,128)(2,1)S(1)}, bf16[1,2048,768]{2,1,0:T(8,128)(2,1)}, u32[]{:S(2)}) copy-start(bf16[1,2048,768]{2,1,0:T(8,128)(2,1)} %param.14) | copy-start | bytes 9437188
  117.4 2.6 %copy-start.2 = (bf16[32,24,2176]{2,1,0:T(8,128)(2,1)S(1)}, bf16[32,24,2176]{2,1,0:T(8,128)(2,1)}, u32[]{:S(2)}) copy-start(bf16[32,24,2176]{2,1,0:T(8,128)(2,1)} %copy-done.1) | copy-start | bytes 10027012
  120.1 1.9 copy-start.15
  125.4 2.7 %copy-start.17 = (bf16[768,768]{1,0:T(8,128)(2,1)}, bf16[768,768]{1,0:T(8,128)(2,1)S(1)}, u32[]{:S(2)}) copy-start(bf16[768,768]{1,0:T(8,128)(2,1)S(1)} %get-tuple-element.19) | copy-start | bytes 3538948
  125.4 2.7 %copy-start.19 = (bf16[768,768]{1,0:T(8,128)(2,1)}, bf16[768,768]{1,0:T(8,128)(2,1)S(1)}, u32[]{:S(2)}) copy-start(bf16[768,768]{1,0:T(8,128)(2,1)S(1)} %get-tuple-element.20) | copy-start | bytes 3538948
  125.4 6.2 %copy-start.21 = (bf16[768,768]{1,0:T(8,128)(2,1)}, bf16[768,768]{1,0:T(8,128)(2,1)S(1)}, u32[]{:S(2)}) copy-start(bf16[768,768]{1,0:T(8,128)(2,1)S(1)} %get-tuple-element.18) | copy-start | bytes 3538948
  125.5 3.2 %copy-start.12 = (bf16[32,24,2048]{2,1,0:T(8,128)(2,1)S(1)}, bf16[32,24,2048]{2,1,0:T(8,128)(2,1)}, u32[]{:S(2)}) copy-start(bf16[32,24,2048]{2,1,0:T(8,128)(2,1)} %slice.7) | copy-start | bytes 9437188
  135.2 52.9 %copy-start.10 = (bf16[128,2048]{1,0:T(8,128)(2,1)S(1)}, bf16[128,2048]{1,0:T(8,128)(2,1)}, u32[]{:S(2)}) copy-start(bf16[128,2048]{1,0:T(8,128)(2,1)} %param.8) | copy-start | bytes 1572868
  135.2 52.9 %copy-start.13 = (f32[2048]{0:T(1024)S(1)}, f32[2048]{0:T(1024)}, u32[]{:S(2)}) copy-start(f32[2048]{0:T(1024)} %param.10) | copy-start | bytes 24580
  135.2 61.2 %copy-start.14 = (s32[128,4]{0,1:T(4,128)S(1)}, s32[128,4]{0,1:T(4,128)}, u32[]{:S(2)}) copy-start(s32[128,4]{0,1:T(4,128)} %param.11) | copy-start | bytes 6148
  187.2 1.0 copy-start.3
  189.2 27.9 %all-to-all-start = ((f32[32,1,64]{2,1,0:T(1,128)}), f32[32,1,64]{2,1,0:T(1,128)S(1)}, u32[]{:S(2)}, u32[]{:S(2)}) async-start(f32[32,1,64]{2,1,0:T(1,128)} %all_to_all.6), calls=%async_computation | async-start | bytes 32768 | tf_op jit(solution)/shard_map/all_to_all | solution.py:481
  197.5 6.7 %copy-start.9 = (bf16[32,24,2048]{2,1,0:T(8,128)(2,1)S(1)}, bf16[32,24,2048]{2,1,0:T(8,128)(2,1)}, u32[]{:S(2)}) copy-start(bf16[32,24,2048]{2,1,0:T(8,128)(2,1)} %copy-done.7) | copy-start | bytes 9437188
  197.5 6.7 %copy-start.18 = (bf16[768,768]{1,0:T(8,128)(2,1)S(1)}, bf16[768,768]{1,0:T(8,128)(2,1)}, u32[]{:S(2)}) copy-start(bf16[768,768]{1,0:T(8,128)(2,1)} %copy-done.17) | copy-start | bytes 3538948
  208.4 2.6 %copy-start.20 = (bf16[768,768]{1,0:T(8,128)(2,1)S(1)}, bf16[768,768]{1,0:T(8,128)(2,1)}, u32[]{:S(2)}) copy-start(bf16[768,768]{1,0:T(8,128)(2,1)} %copy-done.19) | copy-start | bytes 3538948
  211.0 4.1 %copy-start.4 = (f32[128,2048]{1,0:T(8,128)S(1)}, f32[128,2048]{1,0:T(8,128)}, u32[]{:S(2)}) copy-start(f32[128,2048]{1,0:T(8,128)} %copy-done.3) | copy-start | bytes 3145732
  211.0 4.1 %copy-start.6 = (bf16[128,2048]{1,0:T(8,128)(2,1)S(1)}, bf16[128,2048]{1,0:T(8,128)(2,1)}, u32[]{:S(2)}) copy-start(bf16[128,2048]{1,0:T(8,128)(2,1)} %cot.1) | copy-start | bytes 1572868
  211.0 4.0 %copy-start.11 = (bf16[128,2048]{1,0:T(8,128)(2,1)S(1)}, bf16[128,2048]{1,0:T(8,128)(2,1)}, u32[]{:S(2)}) copy-start(bf16[128,2048]{1,0:T(8,128)(2,1)} %param.8) | copy-start | bytes 1572868

commit v4 on v3

--- a/solution.py
+++ b/solution.py
@@ -224,7 +224,8 @@
 
 
 def collect_kernel(
-    seqs, outer, inner, back, table, out_rows, out_grad,
+    seqs, outer, inner, back, table, rows_in, grad_gate, grad_up, act, d_expert,
+    out_rows, out_grad, gate_out, up_out, down_out,
     landed, running, stage, plane_send, plane_recv, own_sem, run_send, run_recv,
 ):
     s, o, i = coords(outer, inner)
@@ -308,8 +309,23 @@
 
     push_all(o)
 
+    def weights(left, right, out):
+        size = 256 if left.shape[1] % 256 == 0 else left.shape[1]
+
+        def one(c, carry):
+            cols = pl.ds(pl.multiple_of(c * size, size), size)
+            out[cols, :] = lax.dot_general(
+                left[:, cols], right[...], turned, preferred_element_type=F32
+            ).astype(BF)
+            return carry
+
+        lax.fori_loop(0, left.shape[1] // size, one, 0)
+
+    work = [(rows_in, grad_gate, gate_out), (rows_in, grad_up, up_out), (act, d_expert, down_out)]
     more = (o < outer - 1, o > 0)
     for j in range(outer - 1, 0, -1):
+        if work:
+            weights(*work.pop(0))
         for src, here, way in cases(j):
 
             @pl.when(here)
@@ -337,6 +353,8 @@
 
                 run_copy(src, way).start()
 
+    while work:
+        weights(*work.pop(0))
     await_all(o)
 
     def mine(cols):
@@ -372,7 +390,7 @@
         lax.fori_loop(1, plane, finish, 0)
 
 
-def collect(back, table, seqs, outer, inner):
+def collect(back, table, parts, seqs, outer, inner):
     count, cap, wide = back.shape
     plane = seqs * inner
     rows = table.shape[2]
@@ -383,9 +401,12 @@
         out_shape=(
             jax.ShapeDtypeStruct((rows, wide - LANES), F32),
             jax.ShapeDtypeStruct((rows, LANES), F32),
+        ) + tuple(
+            jax.ShapeDtypeStruct((a.shape[1], b.shape[1]), BF)
+            for a, b in ((parts[0], parts[1]), (parts[0], parts[2]), (parts[3], parts[4]))
         ),
-        in_specs=[pl.BlockSpec(memory_space=pl.ANY), vmem],
-        out_specs=(vmem, vmem),
+        in_specs=[pl.BlockSpec(memory_space=pl.ANY)] + [vmem] * 6,
+        out_specs=(vmem,) * 5,
         scratch_shapes=[
             pltpu.VMEM((outer, plane, cap, wide), BF),
             pltpu.VMEM((outer, 2, rows, wide), BF),
@@ -397,10 +418,10 @@
             dma((outer, 2)),
         ],
         compiler_params=pltpu.CompilerParams(
-            collective_id=1, has_side_effects=True, vmem_limit_bytes=40 * 1024 * 1024
+            collective_id=1, has_side_effects=True, vmem_limit_bytes=56 * 1024 * 1024
         ),
         name="collect",
-    )(back, table)
+    )(back, table, *parts)
 
 
 def expert_backward(rows_in, rows_cot, rows_gate, gate_w, up_w, down_w):
@@ -415,16 +436,12 @@
     d_act = lax.dot_general(d_expert, down_w, (((1,), (1,)), ((), ())), preferred_element_type=F32)
     grad_gate = (d_act * pre_up * sigmoid_gate * (1.0 + pre_gate * (1.0 - sigmoid_gate))).astype(BF)
     grad_up = (d_act * silu_gate).astype(BF)
-    turned = (((0,), (0,)), ((), ()))
-    grad_down_w = lax.dot_general(act, d_expert, turned, preferred_element_type=F32).astype(BF)
-    grad_gate_w = lax.dot_general(rows_in, grad_gate, turned, preferred_element_type=F32).astype(BF)
-    grad_up_w = lax.dot_general(rows_in, grad_up, turned, preferred_element_type=F32).astype(BF)
     across = (((1,), (1,)), ((), ()))
     d_rows = (
         lax.dot_general(grad_gate, gate_w, across, preferred_element_type=F32)
         + lax.dot_general(grad_up, up_w, across, preferred_element_type=F32)
     ).astype(BF)
-    return (d_rows, slot_grad, grad_gate_w, grad_up_w, grad_down_w)
+    return (d_rows, slot_grad, (rows_in, grad_gate, grad_up, act, d_expert))
 
 
 def body(hidden_in, d_output, gain, route_ids, gates, w_gate, w_up, w_down):
@@ -461,7 +478,7 @@
         .reshape(outer, seqs * inner * cap, tok_rows)
     )
     got_in, got_cot, tables = dispatch(normed, d_output, by_plane, seqs, outer, inner, cap)
-    d_rows, slot_grad, grad_gate_w, grad_up_w, grad_down_w = expert_backward(
+    d_rows, slot_grad, parts = expert_backward(
         got_in.reshape(-1, width), got_cot[:, :, :width].reshape(-1, width),
         got_cot[:, :, width].reshape(-1),
         w_gate[0], w_up[0], w_down[0],
@@ -469,7 +486,9 @@
     back = jnp.concatenate(
         [d_rows, jnp.broadcast_to(slot_grad[:, None], (slot_grad.shape[0], LANES))], axis=1
     ).reshape(devices, cap, width + LANES)
-    d_normed, grad_map = collect(back, tables, seqs, outer, inner)
+    d_normed, grad_map, grad_gate_w, grad_up_w, grad_down_w = collect(
+        back, tables, parts, seqs, outer, inner
+    )
     lane = jnp.arange(LANES, dtype=jnp.int32)
     ids_column = (
         route_ids // inner % outer * (seqs * inner) + route_ids // per_seq * inner + route_ids % inner

time: 218 us -> 230 us (1.055)
  matrix products: 34.3 us -> 22.6 us
  Pallas kernels: 151 us -> 159 us
  other arithmetic: 13.2 us -> 20 us
  local copies, waits for them, and re-layouts: 10.9 us -> 16 us
  waiting for transfers between devices: 0.01 us -> 3.79 us
    dot_general x3 -> x0, matrix products: 14.8 us -> none  [the longest x1 6.71 us: expert_backward(): lax.dot_general(rows_in, grad_up, turned, preferred_element_type=F32)]
    pallas_call x1, Pallas kernels: 51.9 us -> 59.8 us  [collect(): pl.pallas_call(functools.partial(collect_kernel, seqs, outer, inner), out...]
    unnamed x44 -> x53, local copies, waits for them, and re-layouts: 6.52 us -> 12.3 us
    all_to_all x1, waiting for transfers between devices: 0.01 us -> 3.79 us  [body(): lax.all_to_all(gain_term.reshape(devices, -1), AXES, split_axis=0, concat...]
    convert_element_type x2, other arithmetic: 3.13 us -> 6.91 us  [expert_backward(): (rows_gate.astype(F32)[:, None] * rows_cot.astype(F32)).astype(BF)]
  transfers between devices with their start and end apart: 1 -> 1, of which waited for: 0 -> 1; matrix products, arithmetic and copies ran while one was open for 9% -> 1% of each run, Pallas kernels for 0% -> 0%
where the time goes in v4:
time: 230 us; the launch traced here: 229 us
  Pallas kernels  159 us (69%)
  matrix products  22.6 us (10%)
  other arithmetic  20 us (9%)
  local copies, waits for them, and re-layouts  16 us (7%)
  starting transfers between devices  7.05 us (3%)
  waiting for transfers between devices  3.79 us (2%)
    pallas_call x1, Pallas kernels, dispatch(): pl.pallas_call(functools.partial(dispatch_kernel, seqs, outer, inner), ou...  99.1 us
    pallas_call x1, Pallas kernels, collect(): pl.pallas_call(functools.partial(collect_kernel, seqs, outer, inner), out...  59.8 us
    unnamed x53, local copies, waits for them, and re-layouts  12.3 us
    all_to_all x1, starting transfers between devices, body(): lax.all_to_all(gain_term.reshape(devices, -1), AXES, split_axis=0, concat...  7.05 us
    convert_element_type x2, other arithmetic, expert_backward(): (rows_gate.astype(F32)[:, None] * rows_cot.astype(F32)).astype(BF)  6.91 us
    dot_general x1, matrix products, expert_backward(): lax.dot_general(grad_up, up_w, across, preferred_element_type=F32)  4.94 us
    dot_general x1, matrix products, expert_backward(): lax.dot_general(d_expert, down_w, (((1,), (1,)), ((), ())), preferred_ele...  4.75 us
    dot_general x1, matrix products, expert_backward(): lax.dot_general(grad_gate, gate_w, across, preferred_element_type=F32)  4.61 us
  transfers between devices with their start and end apart: 1, of which 1 were waited for; matrix products, arithmetic and copies ran while one was open for 1% of the time, Pallas kernels for 0%

profile of v4, /device:TPU:0, one launch (start us, length us, event | category | flops | bytes accessed | tf_op | source)
XLA Modules:
  0.0 229.3 jit_solution(10671605939483270815)
XLA Ops:
  0.6 0.8 fusion.29
  1.7 0.7 convert_bitcast_fusion
  2.3 0.7 select_reduce_fusion.1
  3.1 1.2 fusion.25
  4.4 1.2 fusion.18.normed
  5.8 1.0 copy-done.5
  6.8 99.1 %dispatch.1 = (bf16[32,24,2048]{2,1,0:T(8,128)(2,1)S(1)}, bf16[32,24,2176]{2,1,0:T(8,128)(2,1)S(1)}, bf16[4,192,128]{2,1,0:T(8,128)(2,1)S(1)}) custom-call(bf16[128,2048]{1,0:T(8,128)(2,1)S(1)} %fusion.18.normed, bf16[128,2048]{1,0:T(8,128)(2,1)S(1)} %copy-done.5, bf16[4,192,128]{2,1,0:T(8,128)(2,1)S(1)} %fusion.26.table), custom_call_target="tpu_custom_call" | custom-call | tf_op jit(solution)/shard_map/dispatch/pallas_call | solution.py:196
  106.0 2.4 %slice.7 = bf16[32,24,2048]{2,1,0:T(8,128)(2,1)} slice(bf16[32,24,2176]{2,1,0:T(8,128)(2,1)S(1)} %get-tuple-element.14), slice={[0:32], [0:24], [0:2048]} | slice | bytes 6291456 | tf_op jit(solution)/shard_map/slice | solution.py:482
  108.6 1.0 copy-done.3
  109.7 0.8 fusion.28
  110.8 2.6 %fusion = bf16[32,24,2048]{2,1,0:T(8,128)(2,1)S(1)} fusion(f32[32,24]{1,0:T(8,128)S(1)} %bitcast.73, bf16[32,24,2176]{2,1,0:T(8,128)(2,1)} %copy-done.2), kind=kLoop, calls=%fused_computation.3 | loop fusion | flops 4718592 | bytes 6294528 | tf_op jit(solution)/shard_map/convert_element_type | solution.py:435
  113.6 2.6 %fusion.5 = f32[768,768]{1,0:T(8,128)S(1)} fusion(bf16[768,2048]{1,0:T(8,128)(2,1)S(1)} %bitcast.66, bf16[1,2048,768]{2,1,0:T(8,128)(2,1)S(1)} %copy-done), kind=kOutput, calls=%fused_computation.10 | convolution fusion | flops 2415919104 | bytes 8650752 | tf_op jit(solution)/shard_map/dot_general | solution.py:428
  116.2 2.6 %fusion.8 = f32[768,768]{1,0:T(8,128)S(1)} fusion(bf16[768,2048]{1,0:T(8,128)(2,1)S(1)} %bitcast.67, bf16[1,2048,768]{2,1,0:T(8,128)(2,1)S(1)} %copy-done.21), kind=kOutput, calls=%fused_computation.13 | convolution fusion | flops 2415919104 | bytes 8650752 | tf_op jit(solution)/shard_map/dot_general | solution.py:429
  118.9 4.7 %multiply_convert_fusion.1 = (bf16[768,768]{1,0:T(8,128)(2,1)}, bf16[768,768]{1,0:T(8,128)(2,1)S(1)}, bf16[768,768]{1,0:T(8,128)(2,1)}) fusion(f32[768,768]{1,0:T(8,128)S(1)} %fusion.5, f32[768,768]{1,0:T(8,128)S(1)} %fusion.8, bf16[768,2048]{1,0:T(8,128)(2,1)S(1)} %bitcast.72, bf16[1,768,2048]{2,1,0:T(8,128)(2,1)S(1)} %copy-done.23), kind=kOutput, calls=%fused_computation.19 | convolution fusion | flops 2424766464 | bytes 14548992 | tf_op jit(solution)/shard_map/dot_general | solution.py:436
  123.6 1.0 copy-done.13
  124.7 4.6 %fusion.3 = f32[768,2048]{1,0:T(8,128)} fusion(bf16[768,768]{1,0:T(8,128)(2,1)S(1)} %get-tuple-element.25.grad_gate, bf16[1,2048,768]{2,1,0:T(8,128)(2,1)S(1)} %copy-done), kind=kOutput, calls=%fused_computation.8 | convolution fusion | flops 2415919104 | bytes 10616832 | tf_op jit(solution)/shard_map/dot_general | solution.py:441
  129.4 4.3 %fusion.2.d_expert = bf16[768,2048]{1,0:T(8,128)(2,1)} fusion(f32[768]{0:T(1024)S(1)} %reshape.81, bf16[32,24,2176]{2,1,0:T(8,128)(2,1)} %copy-done.2), kind=kLoop, calls=%fused_computation.5 | loop fusion | flops 4718592 | bytes 6294528 | tf_op jit(solution)/shard_map/convert_element_type | solution.py:435
  133.7 4.9 %add_convert_fusion = bf16[768,2048]{1,0:T(8,128)(2,1)S(1)} fusion(f32[768,2048]{1,0:T(8,128)} %fusion.3, bf16[768,768]{1,0:T(8,128)(2,1)S(1)} %copy-done.12, bf16[1,2048,768]{2,1,0:T(8,128)(2,1)S(1)} %copy-done.22), kind=kOutput, calls=%fused_computation.6 | convolution fusion | flops 2419064832 | bytes 13762560 | tf_op jit(solution)/shard_map/dot_general | solution.py:442
  138.7 2.9 %fusion.1 = bf16[768]{0:T(1024)(128)(2,1)S(1)} fusion(bf16[32,24,2048]{2,1,0:T(8,128)(2,1)S(1)} %copy-done.11, bf16[768,768]{1,0:T(8,128)(2,1)S(1)} %copy-done.14, bf16[1,768,2048]{2,1,0:T(8,128)(2,1)S(1)} %copy-done.24), kind=kOutput, calls=%fused_computation.4 | convolution fusion | flops 2420636928 | bytes 7472640 | tf_op jit(solution)/shard_map/dot_general | solution.py:433
  141.9 2.0 pad_maximum_fusion
  143.9 59.8 %collect.1 = (f32[128,2048]{1,0:T(8,128)}, f32[128,128]{1,0:T(8,128)}, bf16[2048,768]{1,0:T(8,128)(2,1)}, bf16[2048,768]{1,0:T(8,128)(2,1)}, bf16[768,2048]{1,0:T(8,128)(2,1)}) custom-call(bf16[32,24,2176]{2,1,0:T(8,128)(2,1)} %bitcast.68, bf16[4,192,128]{2,1,0:T(8,128)(2,1)} %copy-done.7, bf16[768,2048]{1,0:T(8,128)(2,1)} %bitcast.65, ...), custom_call_target="tpu_custom_call" | custom-call | tf_op jit(solution)/shard_map/collect/pallas_call | solution.py:399
  203.8 1.6 fusion.24
  205.4 0.7 all_to_all.6
  206.1 7.0 %all-to-all-start = ((f32[32,1,64]{2,1,0:T(1,128)}), f32[32,1,64]{2,1,0:T(1,128)S(1)}, u32[]{:S(2)}, u32[]{:S(2)}) async-start(f32[32,1,64]{2,1,0:T(1,128)} %all_to_all.6), calls=%async_computation | async-start | bytes 32768 | tf_op jit(solution)/shard_map/all_to_all | solution.py:500
  213.2 2.4 %fusion.23 = bf16[128,2048]{1,0:T(8,128)(2,1)} fusion(bf16[128,2048]{1,0:T(8,128)(2,1)S(1)} %copy-done.8, bf16[128,2048]{1,0:T(8,128)(2,1)S(1)} %copy-done.6, f32[128,2048]{1,0:T(8,128)} %get-tuple-element.17, f32[128]{0:T(128)S(1)} %broadcast_multiply_fusion, f32[2048]{0:T(1024)S(1)} %copy-done.15, f32[128]{0:T(128)S(1)} %copy-done.20), kind=kLoop, calls=%fused_computation.35 | loop fusion | flops 2359296 | bytes 2630656 | tf_op jit(solution)/shard_map/convert_element_type | solution.py:508
  215.6 0.8 select_reduce_fusion
  216.4 3.8 %all-to-all-done = f32[32,1,64]{2,1,0:T(1,128)S(1)} async-done(((f32[32,1,64]{2,1,0:T(1,128)}), f32[32,1,64]{2,1,0:T(1,128)S(1)}, u32[]{:S(2)}, u32[]{:S(2)}) %all-to-all-start) | async-done | bytes 8224 | tf_op jit(solution)/shard_map/all_to_all | solution.py:500
  220.2 0.5 reduce_sum.68
  220.7 3.9 %copy.43 = bf16[1,2048,768]{2,1,0:T(8,128)(2,1)} copy(bf16[1,2048,768]{2,1,0:T(8,128)(2,1)} %bitcast.71) | data formatting | bytes 6291456
  224.7 1.7 copy.44
  226.3 1.4 copy-done.9
  227.7 1.7 copy.45
  (58 shorter events, 1.6 us)
Async XLA Ops:
  0.6 112.8 %copy-start = (bf16[1,2048,768]{2,1,0:T(8,128)(2,1)S(1)}, bf16[1,2048,768]{2,1,0:T(8,128)(2,1)}, u32[]{:S(2)}) copy-start(bf16[1,2048,768]{2,1,0:T(8,128)(2,1)} %param.13) | copy-start | bytes 9437188
  4.4 1.2 copy-start.19
  5.8 1.0 copy-start.5
  106.0 2.7 %copy-start.2 = (bf16[32,24,2176]{2,1,0:T(8,128)(2,1)}, bf16[32,24,2176]{2,1,0:T(8,128)(2,1)S(1)}, u32[]{:S(2)}) copy-start(bf16[32,24,2176]{2,1,0:T(8,128)(2,1)S(1)} %get-tuple-element.14) | copy-start | bytes 10027012
  106.0 3.7 %copy-start.3 = (bf16[32,24,2048]{2,1,0:T(8,128)(2,1)}, bf16[32,24,2048]{2,1,0:T(8,128)(2,1)S(1)}, u32[]{:S(2)}) copy-start(bf16[32,24,2048]{2,1,0:T(8,128)(2,1)S(1)} %get-tuple-element.15) | copy-start | bytes 9437188
  106.0 3.7 %copy-start.7 = (bf16[4,192,128]{2,1,0:T(8,128)(2,1)}, bf16[4,192,128]{2,1,0:T(8,128)(2,1)S(1)}, u32[]{:S(2)}) copy-start(bf16[4,192,128]{2,1,0:T(8,128)(2,1)S(1)} %get-tuple-element.16.table) | copy-start | bytes 589828
  110.7 2.9 %copy-start.4 = (bf16[32,24,2048]{2,1,0:T(8,128)(2,1)S(1)}, bf16[32,24,2048]{2,1,0:T(8,128)(2,1)}, u32[]{:S(2)}) copy-start(bf16[32,24,2048]{2,1,0:T(8,128)(2,1)} %copy-done.3) | copy-start | bytes 9437188
  113.6 2.6 %copy-start.21 = (bf16[1,2048,768]{2,1,0:T(8,128)(2,1)S(1)}, bf16[1,2048,768]{2,1,0:T(8,128)(2,1)}, u32[]{:S(2)}) copy-start(bf16[1,2048,768]{2,1,0:T(8,128)(2,1)} %param.14) | copy-start | bytes 9437188
  116.2 2.6 %copy-start.23 = (bf16[1,768,2048]{2,1,0:T(8,128)(2,1)S(1)}, bf16[1,768,2048]{2,1,0:T(8,128)(2,1)}, u32[]{:S(2)}) copy-start(bf16[1,768,2048]{2,1,0:T(8,128)(2,1)} %param.15) | copy-start | bytes 9437188
  123.6 1.0 copy-start.13
  124.7 4.6 %copy-start.17 = (f32[32,24]{1,0:T(8,128)S(1)}, f32[32,24]{1,0:T(8,128)}, u32[]{:S(2)}) copy-start(f32[32,24]{1,0:T(8,128)} %fusion.28) | copy-start | bytes 9220
  129.4 4.3 %copy-start.12 = (bf16[768,768]{1,0:T(8,128)(2,1)S(1)}, bf16[768,768]{1,0:T(8,128)(2,1)}, u32[]{:S(2)}) copy-start(bf16[768,768]{1,0:T(8,128)(2,1)} %get-tuple-element.24.grad_up) | copy-start | bytes 3538948
  129.4 4.3 %copy-start.22 = (bf16[1,2048,768]{2,1,0:T(8,128)(2,1)S(1)}, bf16[1,2048,768]{2,1,0:T(8,128)(2,1)}, u32[]{:S(2)}) copy-start(bf16[1,2048,768]{2,1,0:T(8,128)(2,1)} %param.14) | copy-start | bytes 9437188
  133.7 5.0 %copy-start.11 = (bf16[32,24,2048]{2,1,0:T(8,128)(2,1)S(1)}, bf16[32,24,2048]{2,1,0:T(8,128)(2,1)}, u32[]{:S(2)}) copy-start(bf16[32,24,2048]{2,1,0:T(8,128)(2,1)} %slice.7) | copy-start | bytes 9437188
  133.7 5.0 %copy-start.14 = (bf16[768,768]{1,0:T(8,128)(2,1)S(1)}, bf16[768,768]{1,0:T(8,128)(2,1)}, u32[]{:S(2)}) copy-start(bf16[768,768]{1,0:T(8,128)(2,1)} %get-tuple-element.26.act) | copy-start | bytes 3538948
  133.7 5.1 %copy-start.24 = (bf16[1,768,2048]{2,1,0:T(8,128)(2,1)S(1)}, bf16[1,768,2048]{2,1,0:T(8,128)(2,1)}, u32[]{:S(2)}) copy-start(bf16[1,768,2048]{2,1,0:T(8,128)(2,1)} %param.15) | copy-start | bytes 9437188
  143.9 59.9 %copy-start.8 = (bf16[128,2048]{1,0:T(8,128)(2,1)S(1)}, bf16[128,2048]{1,0:T(8,128)(2,1)}, u32[]{:S(2)}) copy-start(bf16[128,2048]{1,0:T(8,128)(2,1)} %param.8) | copy-start | bytes 1572868
  143.9 59.9 %copy-start.15 = (f32[2048]{0:T(1024)S(1)}, f32[2048]{0:T(1024)}, u32[]{:S(2)}) copy-start(f32[2048]{0:T(1024)} %param.10) | copy-start | bytes 24580
  143.9 59.9 %copy-start.20 = (f32[128]{0:T(128)S(1)}, f32[128]{0:T(128)}, u32[]{:S(2)}) copy-start(f32[128]{0:T(128)} %copy-done.19) | copy-start | bytes 1540
  143.9 69.2 %copy-start.18 = (s32[128,4]{0,1:T(4,128)S(1)}, s32[128,4]{0,1:T(4,128)}, u32[]{:S(2)}) copy-start(s32[128,4]{0,1:T(4,128)} %param.11) | copy-start | bytes 6148
  143.9 69.3 %copy-start.6 = (bf16[128,2048]{1,0:T(8,128)(2,1)S(1)}, bf16[128,2048]{1,0:T(8,128)(2,1)}, u32[]{:S(2)}) copy-start(bf16[128,2048]{1,0:T(8,128)(2,1)} %cot.1) | copy-start | bytes 1572868
  203.7 11.9 %copy-start.16 = (f32[128,128]{1,0:T(8,128)S(1)}, f32[128,128]{1,0:T(8,128)}, u32[]{:S(2)}) copy-start(f32[128,128]{1,0:T(8,128)} %get-tuple-element.18) | copy-start | bytes 196612
  206.1 14.1 %all-to-all-start = ((f32[32,1,64]{2,1,0:T(1,128)}), f32[32,1,64]{2,1,0:T(1,128)S(1)}, u32[]{:S(2)}, u32[]{:S(2)}) async-start(f32[32,1,64]{2,1,0:T(1,128)} %all_to_all.6), calls=%async_computation | async-start | bytes 32768 | tf_op jit(solution)/shard_map/all_to_all | solution.py:500
  220.7 3.9 %copy-start.10 = (bf16[2048,768]{1,0:T(8,128)(2,1)S(1)}, bf16[2048,768]{1,0:T(8,128)(2,1)}, u32[]{:S(2)}) copy-start(bf16[2048,768]{1,0:T(8,128)(2,1)} %get-tuple-element.20) | copy-start | bytes 9437188
  224.6 3.0 %copy-start.9 = (bf16[768,2048]{1,0:T(8,128)(2,1)S(1)}, bf16[768,2048]{1,0:T(8,128)(2,1)}, u32[]{:S(2)}) copy-start(bf16[768,2048]{1,0:T(8,128)(2,1)} %get-tuple-element.21) | copy-start | bytes 9437188
  224.7 4.7 %copy-start.1 = (bf16[1,2048,768]{2,1,0:T(8,128)(2,1)S(1)}, bf16[1,2048,768]{2,1,0:T(8,128)(2,1)}, u32[]{:S(2)}) copy-start(bf16[1,2048,768]{2,1,0:T(8,128)(2,1)} %param.13) | copy-start | bytes 9437188
